TPU v7x, 32 devices: a whole 2x2x4 slice. The times are simulated.
32 devices in a mesh: shard: 4 (over y, core), ctx: 2 (over x), tp: 4 (over z).
Axes of the slice: x: 2, y: 2, z: 4, core: 2. Of those that a mesh axis runs over, the one named last changes fastest.
Arguments:
- block_in: bfloat16 [4, 256, 768], P('shard', 'ctx'), may hold values from -6 to 6
- segment_ids: int32 [4, 256], P('shard', 'ctx'), may hold values from 0 to 3, never falling along the last dimension, each value on 1 to 128 neighbouring positions
- out_cotangent: bfloat16 [4, 256, 768], P('shard', 'ctx'), may hold values from -6 to 6
- attn_gain: bfloat16 [768], P('shard'), may hold values from 0.5 to 1.5
- attn_shift: bfloat16 [768], P('shard'), may hold values from -2.5 to 2.5
- qkv_weight: bfloat16 [768, 3, 768], P('shard', None, 'tp'), may hold values from -4 to 4
- qv_bias: bfloat16 [2, 12, 64], P(None, 'tp', 'shard'), may hold values from -2.5 to 2.5
- proj_weight: bfloat16 [768, 768], P('tp', 'shard'), may hold values from -1.75 to 1.75
- proj_bias: bfloat16 [768], P('shard'), may hold values from -3 to 3
- mlp_gain: bfloat16 [768], P('shard'), may hold values from 0.5 to 1.5
- mlp_shift: bfloat16 [768], P('shard'), may hold values from -2.5 to 2.5
- up_weight: bfloat16 [768, 3072], P('shard', 'tp'), may hold values from -0.21875 to 0.21875
- up_bias: bfloat16 [24, 128], P('tp', 'shard'), may hold values from -3 to 3
- down_weight: bfloat16 [3072, 768], P('tp', 'shard'), may hold values from -0.109375 to 0.109375
- down_bias: bfloat16 [768], P('shard'), may hold values from -3 to 3
Outputs:
- block_out: float32 [4, 256, 768], P('shard', 'ctx')
- block_in_grad: float32 [4, 256, 768], P('shard', 'ctx')
- attn_gain_grad: float32 [768], P('shard')
- attn_shift_grad: float32 [768], P('shard')
- qkv_weight_grad: float32 [768, 3, 768], P('shard', None, 'tp')
- qv_bias_grad: float32 [2, 12, 64], P(None, 'tp', 'shard')
- proj_weight_grad: float32 [768, 768], P('tp', 'shard')
- proj_bias_grad: float32 [768], P('shard')
- mlp_gain_grad: float32 [768], P('shard')
- mlp_shift_grad: float32 [768], P('shard')
- up_weight_grad: float32 [768, 3072], P('shard', 'tp')
- up_bias_grad: float32 [24, 128], P('tp', 'shard')
- down_weight_grad: float32 [3072, 768], P('tp', 'shard')
- down_bias_grad: float32 [768], P('shard')
Inputs may be any that keep to these rules, and one draw needn't show every extreme that they name: `segment_ids`: along each row the numbers never fall; each document holds 1 to 128 tokens, and one document of each row holds exactly 128.
All inputs are finite; a program needn't handle non-finite values.
Results may differ from a plain program's by a relative error of at most 0.0095.
Values may be sent and summed in bfloat16 or wider, within the bound.
A program may use at most 64 MiB of HBM per device.

v0:
```python
import jax
import jax.numpy as jnp
from jax import lax
from jax.sharding import PartitionSpec as P

EPSILON = 1e-05
GELU_ROOT = 0.7978845608028654
GELU_CUBIC = 0.044715
SCORE_SCALE = 0.125
NEGATIVE = -1e30


def passed_along(value, axis, steps):
    count = lax.axis_size(axis)
    pairs = [(source, (source + steps) % count) for source in range(count)]
    return lax.ppermute(value, axis, pairs)


def normalize(values, gain_vec, offset):
    center = jnp.mean(values, axis=-1, keepdims=True)
    shifted = values - center
    spread = jnp.mean(shifted * shifted, axis=-1, keepdims=True)
    inverse = lax.rsqrt(spread + EPSILON)
    unit_vals = shifted * inverse
    return (unit_vals, inverse, unit_vals * gain_vec + offset)


def normalize_back(grad_norm, unit_vals, inverse, gain_vec):
    scaled = grad_norm * gain_vec
    mean_first = jnp.mean(scaled, axis=-1, keepdims=True)
    second = jnp.mean(scaled * unit_vals, axis=-1, keepdims=True)
    return inverse * (scaled - mean_first - unit_vals * second)


def gelu_value(pre_gelu):
    return (
        0.5
        * pre_gelu
        * (1.0 + jnp.tanh(GELU_ROOT * (pre_gelu + GELU_CUBIC * pre_gelu * pre_gelu * pre_gelu)))
    )


def gelu_slope(pre_gelu):
    tangent = jnp.tanh(GELU_ROOT * (pre_gelu + GELU_CUBIC * pre_gelu * pre_gelu * pre_gelu))
    return 0.5 * (1.0 + tangent) + 0.5 * pre_gelu * (1.0 - tangent * tangent) * GELU_ROOT * (
        1.0 + 3.0 * GELU_CUBIC * pre_gelu * pre_gelu
    )


def feature_sum(part_sum):
    return lax.psum(part_sum, "tp")


def allowed_pairs(query_pos, query_seg, key_pos, key_seg):
    causal = key_pos[None, :] <= query_pos[:, None]
    same_doc = query_seg[:, :, None] == key_seg[:, None, :]
    return (causal[None] & same_doc)[:, :, None, :]


def pair_grads(query_side, key_side):
    query_vals, query_grad, query_lse, query_delta, query_pos, query_seg = query_side
    key_vals, value_vals, key_pos, key_seg = key_side
    scores = (
        jnp.einsum("rqhd,rkhd->rqhk", query_vals, key_vals, preferred_element_type=jnp.float32)
        * SCORE_SCALE
    )
    allowed = allowed_pairs(query_pos, query_seg, key_pos, key_seg)
    probs = jnp.where(allowed, jnp.exp(scores - query_lse[..., None]), 0.0)
    value_out = jnp.einsum(
        "rqhk,rqhd->rkhd",
        probs.astype(jnp.bfloat16),
        query_grad,
        preferred_element_type=jnp.float32,
    )
    weight_grad = jnp.einsum(
        "rqhd,rkhd->rqhk", query_grad, value_vals, preferred_element_type=jnp.float32
    )
    score_grad = (probs * (weight_grad - query_delta[..., None])).astype(jnp.bfloat16)
    query_out = jnp.einsum(
        "rqhk,rkhd->rqhd", score_grad, key_vals, preferred_element_type=jnp.float32
    )
    key_out = jnp.einsum(
        "rqhk,rqhd->rkhd", score_grad, query_vals, preferred_element_type=jnp.float32
    )
    return (query_out, key_out, value_out)


def body(
    block_in,
    segment_ids,
    out_cotangent,
    attn_gain,
    attn_shift,
    qkv_weight,
    qv_bias,
    proj_weight,
    proj_bias,
    mlp_gain,
    mlp_shift,
    up_weight,
    up_bias,
    down_weight,
    down_bias,
):
    cycle_size = lax.axis_size("ctx")
    cycle_index = lax.axis_index("ctx")
    row_count, row_tokens, model_width = block_in.shape
    piece_len = row_tokens // cycle_size
    token_count = row_count * row_tokens
    gathered = (
        lax.all_gather(attn_gain, "shard", axis=0, tiled=True),
        lax.all_gather(attn_shift, "shard", axis=0, tiled=True),
        lax.all_gather(qkv_weight, "shard", axis=0, tiled=True),
        lax.all_gather(qv_bias, "shard", axis=2, tiled=True),
        lax.all_gather(proj_weight, "shard", axis=1, tiled=True),
        lax.all_gather(proj_bias, "shard", axis=0, tiled=True),
        lax.all_gather(mlp_gain, "shard", axis=0, tiled=True),
        lax.all_gather(mlp_shift, "shard", axis=0, tiled=True),
        lax.all_gather(up_weight, "shard", axis=0, tiled=True),
        lax.all_gather(up_bias, "shard", axis=1, tiled=True),
        lax.all_gather(down_weight, "shard", axis=1, tiled=True),
        lax.all_gather(down_bias, "shard", axis=0, tiled=True),
    )
    (
        gain_one,
        shift_one,
        qkv_full,
        qv_full,
        proj_full,
        proj_offset,
        gain_two,
        shift_two,
        up_full,
        up_offset,
        down_full,
        down_offset,
    ) = gathered
    head_size = qv_full.shape[2]
    head_width = qkv_full.shape[2]
    head_count = head_width // head_size
    all_segments = lax.all_gather(segment_ids, "ctx", axis=1, tiled=True)
    counter = jnp.arange(row_tokens, dtype=jnp.int32)
    local_in, local_cot = (
        lax.all_to_all(block_in, "ctx", split_axis=1, concat_axis=1, tiled=True),
        lax.all_to_all(out_cotangent, "ctx", split_axis=1, concat_axis=1, tiled=True),
    )

    def positions(source):
        return counter // piece_len * row_tokens + source * piece_len + counter % piece_len

    def segments_of(source):
        return jnp.take(all_segments, positions(source), axis=1)

    gain_one_high = gain_one.astype(jnp.float32)
    gain_two_high = gain_two.astype(jnp.float32)
    residual_in = local_in.reshape(token_count, model_width).astype(jnp.float32)
    unit_one, inverse_one, normed = normalize(
        residual_in, gain_one_high, shift_one.astype(jnp.float32)
    )
    normed_one = normed.astype(jnp.bfloat16)
    projected = jnp.einsum("td,dce->tce", normed_one, qkv_full, preferred_element_type=jnp.float32)
    query_bias = qv_full[0].reshape(head_width).astype(jnp.float32)
    value_bias = qv_full[1].reshape(head_width).astype(jnp.float32)
    head_shape = (row_count, row_tokens, head_count, head_size)
    grad_shape = (row_count, row_tokens, head_width)
    pair_shape = (row_count, row_tokens, 2 * head_width)
    queries = (projected[:, 0] + query_bias).astype(jnp.bfloat16).reshape(head_shape)
    key_value = (
        jnp.concatenate([projected[:, 1], projected[:, 2] + value_bias], axis=-1)
        .astype(jnp.bfloat16)
        .reshape(pair_shape)
    )
    own_positions = positions(cycle_index)
    own_segments = segments_of(cycle_index)

    def split_pair(packed):
        return (
            packed[..., :head_width].reshape(head_shape),
            packed[..., head_width:].reshape(head_shape),
        )

    def circle_pass(visit, state):

        def forward_turn(turn_index, carried):
            inner_state, packed = carried
            inner_state = visit(inner_state, packed, (cycle_index - turn_index) % cycle_size)
            packed = passed_along(packed, "ctx", 1)
            return (inner_state, packed)

        state, packed = lax.fori_loop(0, cycle_size - 1, forward_turn, (state, key_value))
        return visit(state, packed, (cycle_index + 1) % cycle_size)

    def block_scores(packed, source):
        key_pos = positions(source)
        key_seg = segments_of(source)
        key_block, value_block = split_pair(packed)
        scores = (
            jnp.einsum("rqhd,rkhd->rqhk", queries, key_block, preferred_element_type=jnp.float32)
            * SCORE_SCALE
        )
        allowed = allowed_pairs(own_positions, own_segments, key_pos, key_seg)
        return (scores, allowed, value_block)

    def reached(source):
        return jnp.min(positions(source)) <= jnp.max(own_positions)

    def gather_stats(softmax_state, packed, source):

        def compute(carried):
            running_max, running_sum = carried
            scores, allowed, value_block = block_scores(packed, source)
            scores = jnp.where(allowed, scores, NEGATIVE)
            new_max = jnp.maximum(running_max, jnp.max(scores, axis=-1))
            weights = jnp.where(allowed, jnp.exp(scores - new_max[..., None]), 0.0)
            running_sum = running_sum * jnp.exp(running_max - new_max) + jnp.sum(weights, axis=-1)
            return (new_max, running_sum)

        return lax.cond(reached(source), compute, lambda carried: carried, softmax_state)

    start_state = (
        jnp.full(head_shape[:3], NEGATIVE, jnp.float32),
        jnp.zeros(head_shape[:3], jnp.float32),
    )
    running_max, running_sum = circle_pass(gather_stats, start_state)
    log_total = running_max + jnp.log(running_sum)

    def gather_mix(accumulated, packed, source):

        def compute(carried):
            scores, allowed, value_block = block_scores(packed, source)
            probs_low = jnp.where(allowed, jnp.exp(scores - log_total[..., None]), 0.0).astype(
                jnp.bfloat16
            )
            return carried + jnp.einsum(
                "rqhk,rkhd->rqhd", probs_low, value_block, preferred_element_type=jnp.float32
            )

        return lax.cond(reached(source), compute, lambda carried: carried, accumulated)

    accumulated = circle_pass(gather_mix, jnp.zeros(head_shape, jnp.float32))
    mixed_heads = accumulated.astype(jnp.bfloat16)
    mixed_flat = mixed_heads.reshape(token_count, head_width)
    residual_mid = (
        residual_in
        + feature_sum(jnp.dot(mixed_flat, proj_full, preferred_element_type=jnp.float32))
        + proj_offset.astype(jnp.float32)
    )
    unit_two, inverse_two, normed = normalize(
        residual_mid, gain_two_high, shift_two.astype(jnp.float32)
    )
    normed_two = normed.astype(jnp.bfloat16)
    pre_gelu = jnp.dot(normed_two, up_full, preferred_element_type=jnp.float32) + up_offset.reshape(
        -1
    ).astype(jnp.float32)
    hidden = gelu_value(pre_gelu).astype(jnp.bfloat16)
    block_out = (
        residual_mid
        + feature_sum(jnp.dot(hidden, down_full, preferred_element_type=jnp.float32))
        + down_offset.astype(jnp.float32)
    )
    cot_low = local_cot.reshape(token_count, model_width)
    cot_high = cot_low.astype(jnp.float32)
    down_offset_grad = jnp.sum(cot_high, axis=0)
    down_weight_grad = jnp.einsum("tf,td->fd", hidden, cot_low, preferred_element_type=jnp.float32)
    pre_grad = jnp.einsum(
        "td,fd->tf", cot_low, down_full, preferred_element_type=jnp.float32
    ) * gelu_slope(pre_gelu)
    up_offset_grad = jnp.sum(pre_grad, axis=0).reshape(up_offset.shape)
    pre_grad_low = pre_grad.astype(jnp.bfloat16)
    up_weight_grad = jnp.einsum(
        "td,tf->df", normed_two, pre_grad_low, preferred_element_type=jnp.float32
    )
    norm_two_grad = feature_sum(
        jnp.einsum("tf,df->td", pre_grad_low, up_full, preferred_element_type=jnp.float32)
    )
    gain_two_grad = jnp.sum(norm_two_grad * unit_two, axis=0)
    shift_two_grad = jnp.sum(norm_two_grad, axis=0)
    mid_grad = cot_high + normalize_back(norm_two_grad, unit_two, inverse_two, gain_two_high)
    proj_offset_grad = jnp.sum(mid_grad, axis=0)
    mid_grad_low = mid_grad.astype(jnp.bfloat16)
    proj_weight_grad = jnp.einsum(
        "te,td->ed", mixed_flat, mid_grad_low, preferred_element_type=jnp.float32
    )
    mixed_grad = (
        jnp.einsum("td,ed->te", mid_grad_low, proj_full, preferred_element_type=jnp.float32)
        .astype(jnp.bfloat16)
        .reshape(head_shape)
    )
    row_delta = jnp.sum(mixed_grad.astype(jnp.float32) * mixed_heads.astype(jnp.float32), axis=-1)
    zero_queries = jnp.zeros(grad_shape, jnp.float32)
    zero_pairs = jnp.zeros(pair_shape, jnp.float32)
    query_side = (queries, mixed_grad, log_total, row_delta, own_positions, own_segments)

    def key_turn(source, packed, carried):
        key_pos = positions(source)
        key_seg = segments_of(source)

        def compute(inputs):
            query_acc, key_acc = inputs
            key_block, value_block = split_pair(packed)
            query_out, key_out, value_out = pair_grads(
                query_side, (key_block, value_block, key_pos, key_seg)
            )
            key_acc = key_acc + jnp.concatenate(
                [key_out.reshape(grad_shape), value_out.reshape(grad_shape)], axis=-1
            )
            return (query_acc + query_out.reshape(grad_shape), key_acc)

        return lax.cond(
            jnp.min(key_pos) <= jnp.max(own_positions), compute, lambda inputs: inputs, carried
        )

    def pass_keys(key_acc):
        return passed_along(key_acc, "ctx", 1)

    def key_back_turn(turn_index, carried):
        packed, query_acc, key_acc = carried
        query_acc, key_acc = key_turn(
            (cycle_index - turn_index) % cycle_size, packed, (query_acc, key_acc)
        )
        packed = passed_along(packed, "ctx", 1)
        return (packed, query_acc, pass_keys(key_acc))

    packed, query_acc, key_acc = lax.fori_loop(
        0, cycle_size - 1, key_back_turn, (key_value, zero_queries, zero_pairs)
    )
    query_acc, key_acc = key_turn((cycle_index + 1) % cycle_size, packed, (query_acc, key_acc))
    key_acc = pass_keys(key_acc)
    query_grad_all = query_acc * SCORE_SCALE
    key_grad_all = key_acc[..., :head_width] * SCORE_SCALE
    value_grad_all = key_acc[..., head_width:]
    qv_grad = jnp.stack(
        [
            jnp.sum(query_grad_all, axis=(0, 1)).reshape(head_count, head_size),
            jnp.sum(value_grad_all, axis=(0, 1)).reshape(head_count, head_size),
        ]
    )
    qkv_grad = (
        jnp.stack([query_grad_all, key_grad_all, value_grad_all], axis=2)
        .astype(jnp.bfloat16)
        .reshape(token_count, 3, head_width)
    )
    qkv_weight_grad = jnp.einsum(
        "td,tce->dce", normed_one, qkv_grad, preferred_element_type=jnp.float32
    )
    norm_one_grad = feature_sum(
        jnp.einsum("tce,dce->td", qkv_grad, qkv_full, preferred_element_type=jnp.float32)
    )
    gain_one_grad = jnp.sum(norm_one_grad * unit_one, axis=0)
    shift_one_grad = jnp.sum(norm_one_grad, axis=0)
    in_grad = mid_grad + normalize_back(norm_one_grad, unit_one, inverse_one, gain_one_high)
    local_grads = (
        gain_one_grad,
        shift_one_grad,
        qkv_weight_grad,
        qv_grad,
        proj_weight_grad,
        proj_offset_grad,
        gain_two_grad,
        shift_two_grad,
        up_weight_grad,
        up_offset_grad,
        down_weight_grad,
        down_offset_grad,
    )
    owned = (
        lax.psum_scatter(local_grads[0], "shard", scatter_dimension=0, tiled=True),
        lax.psum_scatter(local_grads[1], "shard", scatter_dimension=0, tiled=True),
        lax.psum_scatter(local_grads[2], "shard", scatter_dimension=0, tiled=True),
        lax.psum_scatter(local_grads[3], "shard", scatter_dimension=2, tiled=True),
        lax.psum_scatter(local_grads[4], "shard", scatter_dimension=1, tiled=True),
        lax.psum_scatter(local_grads[5], "shard", scatter_dimension=0, tiled=True),
        lax.psum_scatter(local_grads[6], "shard", scatter_dimension=0, tiled=True),
        lax.psum_scatter(local_grads[7], "shard", scatter_dimension=0, tiled=True),
        lax.psum_scatter(local_grads[8], "shard", scatter_dimension=0, tiled=True),
        lax.psum_scatter(local_grads[9], "shard", scatter_dimension=1, tiled=True),
        lax.psum_scatter(local_grads[10], "shard", scatter_dimension=1, tiled=True),
        lax.psum_scatter(local_grads[11], "shard", scatter_dimension=0, tiled=True),
    )
    totals = lax.psum(
        (
            owned[0],
            owned[1],
            owned[2],
            owned[3],
            owned[4],
            owned[5],
            owned[6],
            owned[7],
            owned[8],
            owned[9],
            owned[10],
            owned[11],
        ),
        "ctx",
    )
    block_out = block_out.reshape(row_count, row_tokens, model_width)
    in_grad = in_grad.reshape(row_count, row_tokens, model_width)
    block_out, in_grad = (
        lax.all_to_all(block_out, "ctx", split_axis=1, concat_axis=1, tiled=True),
        lax.all_to_all(in_grad, "ctx", split_axis=1, concat_axis=1, tiled=True),
    )
    return (block_out, in_grad) + tuple(totals)


def solution(mesh):
    return jax.shard_map(
        body,
        mesh=mesh,
        in_specs=(
            P("shard", "ctx", None),
            P("shard", "ctx"),
            P("shard", "ctx", None),
            P("shard"),
            P("shard"),
            P("shard", None, "tp"),
            P(None, "tp", "shard"),
            P("tp", "shard"),
            P("shard"),
            P("shard"),
            P("shard"),
            P("shard", "tp"),
            P("tp", "shard"),
            P("tp", "shard"),
            P("shard"),
        ),
        out_specs=(
            P("shard", "ctx", None),
            P("shard", "ctx", None),
            P("shard"),
            P("shard"),
            P("shard", None, "tp"),
            P(None, "tp", "shard"),
            P("tp", "shard"),
            P("shard"),
            P("shard"),
            P("shard"),
            P("shard", "tp"),
            P("tp", "shard"),
            P("tp", "shard"),
            P("shard"),
        ),
        check_vma=False,
    )
```

profile of v0, /device:TPU:0, one launch (start us, length us, event | category | flops | bytes accessed | tf_op | source)
XLA Modules:
  0.0 385.3 jit_solution(582812667096194485)
XLA Ops:
  12.5 4.2 %all-to-all-start = ((bf16[2,2,24576]{2,1,0:T(2,128)(2,1)}), bf16[2,2,24576]{2,1,0:T(2,128)(2,1)S(1)}, u32[]{:S(2)}, u32[]{:S(2)}) async-start(bf16[2,2,24576]{2,1,0:T(2,128)(2,1)} %reshape.1015), calls=%async_computation | async-start | bytes 393216 | tf_op jit(solution)/shard_map/all_to_all | solution.py:144
  17.4 4.5 %all_gather.39 = s32[1,256]{1,0:T(1,128)S(1)} all-gather(s32[1,128]{1,0:T(1,128)S(1)} %copy-done.32), channel_id=1, replica_groups=mesh['shard'=4,'ctx'=2,'tp'=4] {'ctx'}, dimensions={1}, use_global_device_ids=true | all-gather | bytes 1536 | tf_op jit(solution)/shard_map/all_gather | solution.py:141
  27.9 11.0 %all-reduce.16 = (bf16[768]{0:T(1024)(128)(2,1)S(1)}, bf16[768]{0:T(1024)(128)(2,1)S(1)}, bf16[768]{0:T(1024)(128)(2,1)S(1)}, bf16[768]{0:T(1024)(128)(2,1)S(1)}...) all-reduce(bf16[768]{0:T(1024)(128)(2,1)S(1)} %dynamic-update-slice, ...), channel_id=1, replica_groups=mesh['shard'=4,'ctx'=2,'tp'=4] {'shard'}, use_global_device_ids=true, to_apply=%add.1 | all-reduce | flops 4608 | bytes 18432
  40.3 5.2 %all_gather.43 = bf16[2,3,64]{1,0,2:T(2,128)(2,1)S(1)} all-gather(bf16[2,3,16]{1,0,2:T(2,128)(2,1)S(1)} %copy.115), channel_id=1, replica_groups=mesh['shard'=4,'ctx'=2,'tp'=4] {'shard'}, dimensions={2}, use_global_device_ids=true | all-gather | bytes 960 | tf_op jit(solution)/shard_map/all_gather | solution.py:114
  46.3 13.0 %all_gather.42 = bf16[768,3,192]{2,1,0:T(4,128)(2,1)S(1)} all-gather(bf16[192,3,192]{2,1,0:T(4,128)(2,1)S(1)} %copy.113), channel_id=1, replica_groups=mesh['shard'=4,'ctx'=2,'tp'=4] {'shard'}, dimensions={0}, use_global_device_ids=true | all-gather | bytes 1105920 | tf_op jit(solution)/shard_map/all_gather | solution.py:113
  60.1 6.6 %all_gather.44 = bf16[192,768]{0,1:T(8,128)(2,1)S(1)} all-gather(bf16[192,192]{0,1:T(8,128)(2,1)S(1)} %copy.118), channel_id=1, replica_groups=mesh['shard'=4,'ctx'=2,'tp'=4] {'shard'}, dimensions={1}, use_global_device_ids=true | all-gather | bytes 368640 | tf_op jit(solution)/shard_map/all_gather | solution.py:115
  75.4 2.5 conditional.8
  78.0 2.5 conditional.9
  83.2 1.9 reduce.9
  85.8 3.4 all-to-all-start.2
  92.6 5.2 %all-gather = bf16[4,32,6]{1,2,0:T(8,128)(2,1)S(1)} all-gather(bf16[1,32,6]{1,2,0:T(8,128)(2,1)S(1)} %bitcast.463), channel_id=1, replica_groups=mesh['shard'=4,'ctx'=2,'tp'=4] {'shard'}, dimensions={0}, use_global_device_ids=true | all-gather | bytes 1920 | tf_op jit(solution)/shard_map/all_gather | solution.py:120
  98.8 21.3 %all-reduce.22.cloned.1.call-done = f32[128,768]{1,0:T(8,128)} async-done(((f32[128,768]{1,0:T(8,128)}), f32[128,768]{1,0:T(8,128)}) %all-reduce.22.cloned.1.call-update) | async-done | bytes 393232 | tf_op jit(solution)/shard_map/psum | solution.py:51
  123.2 2.4 fusion.151
  128.6 35.2 %all-reduce.24.cloned.1.call-done = f32[128,768]{1,0:T(8,128)} async-done(((f32[128,768]{1,0:T(8,128)}), f32[128,768]{1,0:T(8,128)}) %all-reduce.24.cloned.1.call-update) | async-done | bytes 393232 | tf_op jit(solution)/shard_map/psum | solution.py:51
  170.5 3.3 conditional.10
  175.9 3.6 collective-permute-done.1
  179.6 3.3 conditional.11
  184.3 4.3 %collective-permute-done.2 = f32[1,128,384]{1,2,0:T(8,128)S(1)} collective-permute-done((f32[1,128,384]{1,2,0:T(8,128)S(1)}, f32[1,128,384]{1,2,0:T(8,128)S(1)}, u32[]{:S(2)}, u32[]{:S(2)}) %collective-permute-start.2) | collective-permute-done | bytes 196640 | tf_op jit(solution)/shard_map/ppermute | solution.py:16
  188.7 2.0 fusion.103
  191.4 2.0 fusion.110
  193.4 1.9 fusion.100
  195.5 2.5 fusion.131
  202.9 30.3 %reduce-scatter.13.cloned.1.call-done = f32[192,3,192]{2,0,1:T(8,128)} async-done(((f32[768,3,192]{2,0,1:T(8,128)}), f32[192,3,192]{2,0,1:T(8,128)}) %reduce-scatter.13.cloned.1.call-update) | async-done | bytes 442384 | tf_op jit(solution)/shard_map/reduce_scatter | solution.py:369
  233.2 35.5 %reduce-scatter.15.cloned.1.call-done = f32[192,768]{1,0:T(8,128)} async-done(((f32[768,768]{1,0:T(8,128)}), f32[192,768]{1,0:T(8,128)}) %reduce-scatter.15.cloned.1.call-update) | async-done | bytes 589840 | tf_op jit(solution)/shard_map/reduce_scatter | solution.py:375
  268.7 35.7 %reduce-scatter.17.cloned.1.call-done = f32[768,192]{0,1:T(8,128)} async-done(((f32[768,768]{0,1:T(8,128)}), f32[768,192]{0,1:T(8,128)}) %reduce-scatter.17.cloned.1.call-update) | async-done | bytes 589840 | tf_op jit(solution)/shard_map/reduce_scatter | solution.py:377
  306.8 3.5 all-to-all-start.1
  311.9 9.9 %all-to-all-done.1 = f32[1,128,768]{2,0,1:T(1,128)S(1)} async-done(((f32[1,128,768]{2,0,1:T(1,128)}), f32[1,128,768]{2,0,1:T(1,128)S(1)}, u32[]{:S(2)}, u32[]{:S(2)}) %all-to-all-start.1) | async-done | bytes 393248 | tf_op jit(solution)/shard_map/all_to_all | solution.py:400
  321.8 3.5 all-to-all-start.3
  327.6 21.6 %reduce-scatter.19.cloned.1.call-done = f32[16,6]{1,0:T(8,128)} async-done(((f32[64,6]{1,0:T(8,128)}), f32[16,6]{1,0:T(8,128)}) %reduce-scatter.19.cloned.1.call-update) | async-done | bytes 400
  350.1 11.1 %all-reduce.13 = (f32[768]{0:T(1024)S(1)}, f32[768]{0:T(1024)S(1)}, f32[768]{0:T(1024)S(1)}, f32[768]{0:T(1024)S(1)}, f32[768]{0:T(1024)S(1)}, /*index=5*/f32[768]{0:T(1024)S(1)}) all-reduce(f32[768]{0:T(1024)S(1)} %get-tuple-element.457, f32[768]{0:T(1024)S(1)} %get-tuple-element.462, ...), channel_id=2, replica_groups=mesh['shard'=4,'ctx'=2,'tp'=4] {'shard'}, use_global_device_ids=true, to_apply=%region_33.35.clone | all-reduce | flops 4608 | bytes 36864
  361.6 9.1 %all-reduce.14 = (f32[192]{0:T(256)}, f32[192]{0:T(256)}, f32[2,3,16]{2,1,0:T(4,128)S(1)}, f32[192]{0:T(256)}, f32[192]{0:T(256)}, /*index=5*/f32[192]{0:T(256)}, f32[6,32]{1,0:T(8,128)}, f32[192]{0:T(256)}) all-reduce(f32[192]{0:T(256)S(1)} %dynamic-slice.7, ...), channel_id=1, replica_groups=mesh['shard'=4,'ctx'=2,'tp'=4] {'ctx'}, use_global_device_ids=true, to_apply=%region_34.36 | all-reduce | flops 1440 | bytes 11520 | tf_op jit(solution)/shard_map/psum | solution.py:380
  373.8 2.0 copy.192
  (295 shorter events, 75.9 us)
Async XLA Ops:
  8.1 19.5 %copy-start.38 = (bf16[192]{0:T(256)(128)(2,1)S(1)}, bf16[192]{0:T(256)(128)(2,1)}, u32[]{:S(2)}) copy-start(bf16[192]{0:T(256)(128)(2,1)} %param.43) | copy-start | bytes 1156
  9.4 30.8 %copy-start.31 = (bf16[2,3,16]{2,0,1:T(2,128)(2,1)S(1)}, bf16[2,3,16]{2,0,1:T(2,128)(2,1)}, u32[]{:S(2)}) copy-start(bf16[2,3,16]{2,0,1:T(2,128)(2,1)} %param.35) | copy-start | bytes 580
  9.4 36.5 %copy-start.12 = (bf16[192,192]{1,0:T(8,128)(2,1)S(1)}, bf16[192,192]{1,0:T(8,128)(2,1)}, u32[]{:S(2)}) copy-start(bf16[192,192]{1,0:T(8,128)(2,1)} %param.36) | copy-start | bytes 221188
  9.9 36.1 %copy-start.9 = (bf16[192,3,192]{2,0,1:T(8,128)(2,1)S(1)}, bf16[192,3,192]{2,0,1:T(8,128)(2,1)}, u32[]{:S(2)}) copy-start(bf16[192,3,192]{2,0,1:T(8,128)(2,1)} %param.34) | copy-start | bytes 663556
  12.5 54.2 %all-to-all-start = ((bf16[2,2,24576]{2,1,0:T(2,128)(2,1)}), bf16[2,2,24576]{2,1,0:T(2,128)(2,1)S(1)}, u32[]{:S(2)}, u32[]{:S(2)}) async-start(bf16[2,2,24576]{2,1,0:T(2,128)(2,1)} %reshape.1015), calls=%async_computation | async-start | bytes 393216 | tf_op jit(solution)/shard_map/all_to_all | solution.py:144
  16.7 103.4 %all-reduce.22.cloned.1.call-start = ((), (), s32[]{:S(2)}) async-start(), calls=%async_computation.10 | async-start | bytes 786432 | tf_op jit(solution)/shard_map/psum | solution.py:51
  17.3 60.7 %copy-start.13 = (s32[128]{0:T(128)}, s32[128]{0:T(128)S(1)}, u32[]{:S(2)}) copy-start(s32[128]{0:T(128)S(1)} %add_add_fusion.1) | copy-start | bytes 1540
  40.2 37.8 %copy-start.14 = (s32[1,128]{1,0:T(1,128)}, s32[1,128]{1,0:T(1,128)S(1)}, u32[]{:S(2)}) copy-start(s32[1,128]{1,0:T(1,128)S(1)} %fusion.120) | copy-start | bytes 1540
  67.9 5.1 %collective-permute-start = (bf16[1,128,384]{1,2,0:T(8,128)(2,1)S(1)}, bf16[1,128,384]{1,2,0:T(8,128)(2,1)S(1)}, u32[]{:S(2)}, u32[]{:S(2)}) collective-permute-start(bf16[1,128,384]{1,2,0:T(8,128)(2,1)S(1)} %pad_maximum_fusion.1), channel_id=1, source_target_pairs={{0,4},{4,0},{1,5},{5,1},{2,6},{6,2},{3,7},{7,3},{8,12},{12,8},{9,1... | collective-permute-start | bytes 294920 | tf_op jit(solution)/shard_map/while/body/eval_jaxpr/ppermute | solution.py:16
  81.7 39.8 %all-gather.4.cloned.1.call-start = ((), (), s32[]{:S(2)}) async-start(), calls=%async_computation.11 | async-start | bytes 1474560 | tf_op jit(solution)/shard_map/all_gather | solution.py:119
  82.2 40.9 %all-gather.6.cloned.1.call-start = ((), (), s32[]{:S(2)}) async-start(), calls=%async_computation.12 | async-start | bytes 1474560 | tf_op jit(solution)/shard_map/all_gather | solution.py:121
  85.8 12.2 %all-to-all-start.2 = ((bf16[2,2,24576]{2,1,0:T(2,128)(2,1)}), bf16[2,2,24576]{2,1,0:T(2,128)(2,1)S(1)}, u32[]{:S(2)}, u32[]{:S(2)}) async-start(bf16[2,2,24576]{2,1,0:T(2,128)(2,1)} %reshape.1017), calls=%async_computation.2 | async-start | bytes 393216 | tf_op jit(solution)/shard_map/all_to_all | solution.py:145
  89.2 74.6 %all-reduce.24.cloned.1.call-start = ((), (), s32[]{:S(2)}) async-start(), calls=%async_computation.13 | async-start | bytes 786432 | tf_op jit(solution)/shard_map/psum | solution.py:51
  121.3 44.4 %copy-start.21 = (f32[128]{0:T(128)}, f32[128]{0:T(128)S(1)}, u32[]{:S(2)}) copy-start(f32[128]{0:T(128)S(1)} %broadcast_multiply_fusion.4) | copy-start | bytes 1540
  121.5 44.2 %copy-start.25 = (f32[128]{0:T(128)}, f32[128]{0:T(128)S(1)}, u32[]{:S(2)}) copy-start(f32[128]{0:T(128)S(1)} %add_rsqrt_fusion) | copy-start | bytes 1540
  127.0 74.2 %reduce-scatter.21.cloned.1.call-start = ((), (), s32[]{:S(2)}) async-start(), calls=%async_computation.18 | async-start | bytes 983040
  173.8 5.7 %collective-permute-start.1 = (f32[1,128,384]{1,2,0:T(8,128)S(1)}, f32[1,128,384]{1,2,0:T(8,128)S(1)}, u32[]{:S(2)}, u32[]{:S(2)}) collective-permute-start(f32[1,128,384]{1,2,0:T(8,128)S(1)} %get-tuple-element.376), channel_id=1, source_target_pairs={{0,4},{4,0},{1,5},{5,1},{2,6},{6,2},{3,7},{7,3},{8,12},{12,8},{9,1... | collective-permute-start | bytes 589832 | tf_op jit(solution)/shard_map/while/body/eval_jaxpr/ppermute | solution.py:16
  175.2 58.0 %reduce-scatter.13.cloned.1.call-start = ((), (), s32[]{:S(2)}) async-start(), calls=%async_computation.14 | async-start | bytes 2949120 | tf_op jit(solution)/shard_map/reduce_scatter | solution.py:369
  182.8 5.7 %collective-permute-start.2 = (f32[1,128,384]{1,2,0:T(8,128)S(1)}, f32[1,128,384]{1,2,0:T(8,128)S(1)}, u32[]{:S(2)}, u32[]{:S(2)}) collective-permute-start(f32[1,128,384]{1,2,0:T(8,128)S(1)} %get-tuple-element.378), channel_id=1, source_target_pairs={{0,4},{4,0},{1,5},{5,1},{2,6},{6,2},{3,7},{7,3},{8,12},{12,8},{9,1... | collective-permute-start | bytes 589832 | tf_op jit(solution)/shard_map/ppermute | solution.py:16
  190.8 77.9 %reduce-scatter.15.cloned.1.call-start = ((), (), s32[]{:S(2)}) async-start(), calls=%async_computation.15 | async-start | bytes 2949120 | tf_op jit(solution)/shard_map/reduce_scatter | solution.py:375
  193.4 111.0 %reduce-scatter.17.cloned.1.call-start = ((), (), s32[]{:S(2)}) async-start(), calls=%async_computation.16 | async-start | bytes 2949120 | tf_op jit(solution)/shard_map/reduce_scatter | solution.py:377
  195.4 109.1 %all-reduce.26.cloned.1.call-start = ((), (), s32[]{:S(2)}) async-start(), calls=%async_computation.20 | async-start | bytes 1572864 | tf_op jit(solution)/shard_map/psum | solution.py:51
  199.1 127.7 %reduce-scatter.23.cloned.1.call-start = ((), (), s32[]{:S(2)}) async-start(), calls=%async_computation.19 | async-start | bytes 81920
  199.9 149.2 %reduce-scatter.19.cloned.1.call-start = ((), (), s32[]{:S(2)}) async-start(), calls=%async_computation.17 | async-start | bytes 40960
  201.0 172.8 %all-reduce.28.cloned.1.call-start = ((), (), s32[]{:S(2)}) async-start(), calls=%async_computation.21 | async-start | bytes 3932160 | tf_op jit(solution)/shard_map/psum | solution.py:380
  201.1 103.3 %copy-start.29 = (bf16[768]{0:T(1024)(128)(2,1)S(1)}, bf16[768]{0:T(1024)(128)(2,1)}, u32[]{:S(2)}) copy-start(bf16[768]{0:T(1024)(128)(2,1)} %get-tuple-element.488) | copy-start | bytes 4612
  306.8 15.1 %all-to-all-start.1 = ((f32[1,128,768]{2,0,1:T(1,128)}), f32[1,128,768]{2,0,1:T(1,128)S(1)}, u32[]{:S(2)}, u32[]{:S(2)}) async-start(f32[1,128,768]{2,0,1:T(1,128)} %copy.120), calls=%async_computation.1 | async-start | bytes 786432 | tf_op jit(solution)/shard_map/all_to_all | solution.py:400
  310.5 39.5 %copy-start.15 = (f32[768]{0:T(1024)S(1)}, f32[768]{0:T(1024)}, u32[]{:S(2)}) copy-start(f32[768]{0:T(1024)} %get-tuple-element.499) | copy-start | bytes 9220
  310.5 39.5 %copy-start.16 = (f32[768]{0:T(1024)S(1)}, f32[768]{0:T(1024)}, u32[]{:S(2)}) copy-start(f32[768]{0:T(1024)} %get-tuple-element.455) | copy-start | bytes 9220
  310.5 39.5 %copy-start.17 = (f32[768]{0:T(1024)S(1)}, f32[768]{0:T(1024)}, u32[]{:S(2)}) copy-start(f32[768]{0:T(1024)} %get-tuple-element.461) | copy-start | bytes 9220
  310.5 39.5 %copy-start.18 = (f32[768]{0:T(1024)S(1)}, f32[768]{0:T(1024)}, u32[]{:S(2)}) copy-start(f32[768]{0:T(1024)} %get-tuple-element.501) | copy-start | bytes 9220
  321.8 50.1 %all-to-all-start.3 = ((f32[1,128,768]{2,0,1:T(1,128)}), f32[1,128,768]{2,0,1:T(1,128)S(1)}, u32[]{:S(2)}, u32[]{:S(2)}) async-start(f32[1,128,768]{2,0,1:T(1,128)} %copy.123), calls=%async_computation.3 | async-start | bytes 786432 | tf_op jit(solution)/shard_map/all_to_all | solution.py:401
  (26 other events, 194.3 us)
Sparse Core Ops, SparseCore 0:
  81.8 38.2 all-reduce.21
  127.1 36.6 all-reduce.23
  199.2 43.6 all-reduce.25
  304.6 69.1 all-reduce.27
Sparse Core Ops, SparseCore 1:
  83.8 18.6 all-gather.3
  103.9 17.3 all-gather.5
  175.3 22.1 reduce-scatter.20
  200.1 33.0 reduce-scatter.12
  235.7 32.9 reduce-scatter.14
  271.4 33.0 reduce-scatter.16
  307.3 19.5 reduce-scatter.22
  329.8 19.3 reduce-scatter.18
where the time goes:
time: 386 us; the launch traced here: 385 us
  waiting for transfers between devices  202 us (52%)
  blocking collectives  65.6 us (17%)
  local copies, waits for them, and re-layouts  32.3 us (8%)
  matrix products  25.4 us (7%)
  between operations  20.1 us (5%)
  other arithmetic  19.7 us (5%)
  starting transfers between devices  19.5 us (5%)
    psum x3, waiting for transfers between devices, feature_sum(): return lax.psum(part_sum, 'tp')  56.5 us
    reduce_scatter x1, waiting for transfers between devices, body(): lax.psum_scatter(local_grads[10], 'shard', scatter_dimension=1, tiled=True)  35.7 us
    reduce_scatter x1, waiting for transfers between devices, body(): lax.psum_scatter(local_grads[8], 'shard', scatter_dimension=0, tiled=True)  35.5 us
    reduce_scatter x1, waiting for transfers between devices, body(): lax.psum_scatter(local_grads[2], 'shard', scatter_dimension=0, tiled=True)  30.3 us
    unnamed x15, waiting for transfers between devices  23.7 us
    unnamed x2, blocking collectives  22.1 us
    unnamed x124, local copies, waits for them, and re-layouts  19.2 us
    all_gather x1, blocking collectives, body(): lax.all_gather(qkv_weight, 'shard', axis=0, tiled=True)  13 us
  transfers between devices with their start and end apart: 19, of which 12 were waited for; matrix products, arithmetic and copies ran while one was open for 12% of the time, Pallas kernels for 0%

commit v1 on v0

--- a/solution.py
+++ b/solution.py
@@ -1,6 +1,8 @@
 import jax
 import jax.numpy as jnp
 from jax import lax
+from jax.experimental import pallas as pl
+from jax.experimental.pallas import tpu as pltpu
 from jax.sharding import PartitionSpec as P
 
 EPSILON = 1e-05
@@ -403,9 +405,393 @@
     return (block_out, in_grad) + tuple(totals)
 
 
+MESH = pl.DeviceIdType.MESH
+F32 = jnp.float32
+BF16 = jnp.bfloat16
+GAIN_ONE, SHIFT_ONE, PROJ_BIAS, GAIN_TWO, SHIFT_TWO, DOWN_BIAS, UP_BIAS, Q_BIAS, V_BIAS = range(9)
+VEC_ROWS = 16
+COPIES = 64
+
+
+def mm(left, right, dims=((1,), (0,))):
+    return lax.dot_general(left, right, (dims, ((), ())), preferred_element_type=F32)
+
+
+NT = ((1,), (1,))
+TN = ((0,), (0,))
+
+
+def block_kernel(
+    x_ref, cot_ref, segq_ref, segk_ref, attn_w, up_w, down_w, vec_ref,
+    out_ref, in_grad_ref, attn_g_ref, up_g_ref, down_g_ref, vec_g_ref,
+    attn_f, up_f, down_f, vec_in, segk_in, kv, kv_in, dkv, dkv_in,
+    part, ar_send, ar_recv, ar_all,
+    attn_g, up_g, down_g, attn_s1, attn_r1, attn_s2, attn_r2, attn_s3, attn_r3,
+    mlp_s1, mlp_r1, mlp_s2, mlp_r2, mlp_s3, mlp_r3,
+    vec_s, vec_r, send_sem, recv_sem,
+):
+    shard = lax.axis_index("shard")
+    ctx = lax.axis_index("ctx")
+    tp = lax.axis_index("tp")
+    core = lax.rem(shard, 2)
+    high = shard // 2
+    s1 = shard + 1 - 2 * core
+    s2 = lax.rem(shard + 2, 4)
+    s3 = lax.rem(s1 + 2, 4)
+    p1, p2, p3 = {"shard": s1}, {"shard": s2}, {"shard": s3}
+    pc = {"ctx": 1 - ctx}
+    tps = [lax.rem(tp + step, 4) for step in (1, 2, 3)]
+    tokens, width = x_ref.shape
+    depth = up_w.shape[0]
+    heads_width = attn_w.shape[2]
+    head_count = heads_width // 64
+
+    barrier = pltpu.get_barrier_semaphore()
+    peers = [p1, p2, p3, pc] + [{"tp": t} for t in tps]
+    for peer in peers:
+        pl.semaphore_signal(barrier, inc=1, device_id=peer, device_id_type=MESH)
+
+    started = []
+
+    def send(src, dst, peer):
+        slot = len(started)
+        copy = pltpu.make_async_remote_copy(
+            src_ref=src, dst_ref=dst, send_sem=send_sem.at[slot], recv_sem=recv_sem.at[slot],
+            device_id=peer, device_id_type=MESH,
+        )
+        copy.start()
+        started.append(copy)
+        return copy
+
+    def unit_of(values):
+        center = jnp.mean(values, axis=-1, keepdims=True)
+        shifted = values - center
+        inverse = lax.rsqrt(jnp.mean(shifted * shifted, axis=-1, keepdims=True) + EPSILON)
+        return shifted * inverse, inverse
+
+    pl.semaphore_wait(barrier, len(peers))
+
+    def gather_start(local, full):
+        far = send(local, full.at[shard], p2)
+        near = send(local, full.at[shard], p1)
+        return far, near
+
+    def gather_pass(full, far):
+        far.wait_recv()
+        return send(full.at[s2], full.at[s2], p1)
+
+    attn_far, attn_near = gather_start(attn_w, attn_f)
+    vec_copies = [send(vec_ref, vec_in.at[i], p) for i, p in enumerate((p1, p2, p3))]
+    seg_copy = send(segk_ref, segk_in, pc)
+    attn_f[shard] = attn_w[...]
+    up_f[shard] = up_w[...]
+    down_f[shard] = down_w[...]
+    residual_in = x_ref[...].astype(F32)
+    unit_one, inverse_one = unit_of(residual_in)
+    for copy in vec_copies:
+        copy.wait_recv()
+    vec = vec_ref[...] + vec_in[0] + vec_in[1] + vec_in[2]
+
+    def row(index, size=width):
+        return vec[index : index + 1, :size]
+
+    normed_one = (unit_one * row(GAIN_ONE) + row(SHIFT_ONE)).astype(BF16)
+    attn_pass = gather_pass(attn_f, attn_far)
+    up_far, up_near = gather_start(up_w, up_f)
+    down_far, down_near = gather_start(down_w, down_f)
+    attn_near.wait_recv()
+    attn_pass.wait_recv()
+    weight_q, weight_k, weight_v, weight_p = (
+        attn_f[:, index].reshape(4 * depth, heads_width) for index in range(4)
+    )
+    keys = mm(normed_one, weight_k).astype(BF16)
+    values = (mm(normed_one, weight_v) + row(V_BIAS, heads_width)).astype(BF16)
+    kv[0] = keys
+    kv[1] = values
+    kv_copy = send(kv, kv_in, pc)
+    queries = (mm(normed_one, weight_q) + row(Q_BIAS, heads_width)).astype(BF16)
+
+    lane_head = lax.broadcasted_iota(jnp.int32, (tokens, heads_width), 1) // 64
+    of_head = [lane_head == index for index in range(head_count)]
+
+    def pick(values_in, index):
+        return jnp.where(of_head[index], values_in, jnp.zeros_like(values_in))
+
+    seg_copy.wait_recv()
+    query_at = lax.broadcasted_iota(jnp.int32, (tokens, tokens), 0)
+    key_at = lax.broadcasted_iota(jnp.int32, (tokens, tokens), 1)
+    segq = segq_ref[...]
+    allow_own = (key_at <= query_at) & (segq == segk_ref[0:1, :])
+    allow_other = (segq == segk_in[0:1, :]) & (key_at + tokens * (1 - ctx) <= query_at + tokens * ctx)
+    query_of = [pick(queries, index) for index in range(head_count)]
+    score_own = [
+        jnp.where(allow_own, mm(query_of[i], keys, NT) * SCORE_SCALE, NEGATIVE)
+        for i in range(head_count)
+    ]
+    kv_copy.wait_recv()
+    keys_other = kv_in[0]
+    values_other = kv_in[1]
+    probs_own, probs_other = [], []
+    mixed_sum = jnp.zeros((tokens, heads_width), F32)
+    for i in range(head_count):
+        own = score_own[i]
+        other = jnp.where(allow_other, mm(query_of[i], keys_other, NT) * SCORE_SCALE, NEGATIVE)
+        top = jnp.maximum(
+            jnp.max(own, axis=-1, keepdims=True), jnp.max(other, axis=-1, keepdims=True)
+        )
+        total = jnp.sum(jnp.exp(own - top), axis=-1, keepdims=True) + jnp.sum(
+            jnp.exp(other - top), axis=-1, keepdims=True
+        )
+        log_total = top + jnp.log(total)
+        probs_own.append(jnp.where(allow_own, jnp.exp(own - log_total), 0.0))
+        probs_other.append(jnp.where(allow_other, jnp.exp(other - log_total), 0.0))
+        mixed_head = mm(probs_own[i].astype(BF16), values) + mm(
+            probs_other[i].astype(BF16), values_other
+        )
+        mixed_sum = mixed_sum + pick(mixed_head, i)
+    mixed = mixed_sum.astype(BF16)
+
+    def sum_start(phase, value):
+        pieces = value.reshape(4, tokens // 4, width)
+        part[phase] = pieces
+        ar_send[phase] = pieces.astype(BF16)
+        return [send(ar_send.at[phase, t], ar_recv.at[phase, i], {"tp": t}) for i, t in enumerate(tps)]
+
+    def sum_pass(phase, copies):
+        total = part[phase, tp]
+        for i, copy in enumerate(copies):
+            copy.wait_recv()
+            total = total + ar_recv[phase, i].astype(F32)
+        ar_all[phase, tp] = total.astype(BF16)
+        return [send(ar_all.at[phase, tp], ar_all.at[phase, tp], {"tp": t}) for t in tps]
+
+    def sum_end(phase, copies):
+        for copy in copies:
+            copy.wait_recv()
+        return ar_all[phase].reshape(tokens, width).astype(F32)
+
+    mid_sum = sum_start(0, mm(mixed, weight_p, NT))
+    up_pass = gather_pass(up_f, up_far)
+    mid_sum = sum_pass(0, mid_sum)
+    down_pass = gather_pass(down_f, down_far)
+    residual_mid = residual_in + sum_end(0, mid_sum) + row(PROJ_BIAS)
+    unit_two, inverse_two = unit_of(residual_mid)
+    normed_two = (unit_two * row(GAIN_TWO) + row(SHIFT_TWO)).astype(BF16)
+    up_near.wait_recv()
+    up_pass.wait_recv()
+    up_full = up_f[...].reshape(4 * depth, up_f.shape[2])
+    pre_gelu = mm(normed_two, up_full) + row(UP_BIAS)
+    tangent = jnp.tanh(GELU_ROOT * (pre_gelu + GELU_CUBIC * pre_gelu * pre_gelu * pre_gelu))
+    hidden = (0.5 * pre_gelu * (1.0 + tangent)).astype(BF16)
+    slope = 0.5 * (1.0 + tangent) + 0.5 * pre_gelu * (1.0 - tangent * tangent) * GELU_ROOT * (
+        1.0 + 3.0 * GELU_CUBIC * pre_gelu * pre_gelu
+    )
+    down_near.wait_recv()
+    down_pass.wait_recv()
+    down_full = down_f[...].reshape(4 * depth, down_f.shape[2])
+    cot_low = cot_ref[...]
+    cot_high = cot_low.astype(F32)
+    pre_grad = mm(cot_low, down_full) * slope
+    pre_grad_low = pre_grad.astype(BF16)
+    two_sum = sum_start(2, mm(pre_grad_low, up_full, NT))
+    out_sum = sum_start(1, mm(hidden, down_full, NT))
+
+    def column_sum(value):
+        return jnp.sum(value, axis=0, keepdims=True)
+
+    vec_s[0] = jnp.zeros((VEC_ROWS, width), F32)
+    vec_s[0, UP_BIAS : UP_BIAS + 1, :] = column_sum(pre_grad)
+    vec_s[0, DOWN_BIAS : DOWN_BIAS + 1, :] = column_sum(cot_high)
+
+    def reduce_one(grads, s1_buf, r1_buf):
+        for half in range(2):
+            s1_buf[half] = grads[2 * half + 1 - core].astype(BF16)
+        return send(s1_buf, r1_buf, p1)
+
+    def reduce_two(copy, grads, r1_buf, s2_buf, r2_buf):
+        copy.wait_recv()
+        s2_buf[...] = (grads[s2] + r1_buf[1 - high].astype(F32)).astype(BF16)
+        return send(s2_buf, r2_buf, p2)
+
+    def reduce_three(copy, grads, r1_buf, r2_buf, s3_buf, r3_buf):
+        copy.wait_recv()
+        s3_buf[...] = (
+            grads[shard] + r1_buf[high].astype(F32) + r2_buf[...].astype(F32)
+        ).astype(BF16)
+        return send(s3_buf, r3_buf, pc)
+
+    def reduce_end(copy, s3_buf, r3_buf, result):
+        copy.wait_recv()
+        result[...] = s3_buf[...].astype(F32) + r3_buf[...].astype(F32)
+
+    down_g[...] = mm(cot_low, hidden, TN).reshape(down_g.shape)
+    down_copy = reduce_one(down_g, mlp_s1.at[1], mlp_r1.at[1])
+    two_sum = sum_pass(2, two_sum)
+    up_g[...] = mm(normed_two, pre_grad_low, TN).reshape(up_g.shape)
+    up_copy = reduce_one(up_g, mlp_s1.at[0], mlp_r1.at[0])
+    down_copy = reduce_two(down_copy, down_g, mlp_r1.at[1], mlp_s2.at[1], mlp_r2.at[1])
+    norm_two_grad = sum_end(2, two_sum)
+    vec_s[0, GAIN_TWO : GAIN_TWO + 1, :] = column_sum(norm_two_grad * unit_two)
+    vec_s[0, SHIFT_TWO : SHIFT_TWO + 1, :] = column_sum(norm_two_grad)
+    mid_grad = cot_high + normalize_back(norm_two_grad, unit_two, inverse_two, row(GAIN_TWO))
+    vec_s[0, PROJ_BIAS : PROJ_BIAS + 1, :] = column_sum(mid_grad)
+    mid_grad_low = mid_grad.astype(BF16)
+    mixed_grad = mm(mid_grad_low, weight_p).astype(BF16)
+    delta_terms = mixed_grad.astype(F32) * mixed.astype(F32)
+    zero = jnp.zeros((tokens, heads_width), F32)
+    query_grad, key_own, value_own, key_other, value_other = zero, zero, zero, zero, zero
+    for i in range(head_count):
+        head_grad = pick(mixed_grad, i)
+        delta = jnp.sum(pick(delta_terms, i), axis=-1, keepdims=True)
+        grad_other = (probs_other[i] * (mm(head_grad, values_other, NT) - delta)).astype(BF16)
+        grad_own = (probs_own[i] * (mm(head_grad, values, NT) - delta)).astype(BF16)
+        key_other = key_other + mm(grad_other, query_of[i], TN)
+        value_other = value_other + mm(probs_other[i].astype(BF16), head_grad, TN)
+        key_own = key_own + mm(grad_own, query_of[i], TN)
+        value_own = value_own + mm(probs_own[i].astype(BF16), head_grad, TN)
+        query_grad = query_grad + pick(mm(grad_own, keys) + mm(grad_other, keys_other), i)
+    dkv[0] = key_other.astype(BF16)
+    dkv[1] = value_other.astype(BF16)
+    dkv_copy = send(dkv, dkv_in, pc)
+    up_copy = reduce_two(up_copy, up_g, mlp_r1.at[0], mlp_s2.at[0], mlp_r2.at[0])
+    out_sum = sum_pass(1, out_sum)
+    proj_grad = mm(mid_grad_low, mixed, TN).reshape(4, depth, heads_width)
+    for index in range(4):
+        attn_g[index, 3] = proj_grad[index]
+    query_grad = query_grad * SCORE_SCALE
+    query_low = query_grad.astype(BF16)
+    vec_s[0, Q_BIAS : Q_BIAS + 1, :heads_width] = column_sum(query_grad)
+    one_part = mm(query_low, weight_q, NT)
+    dkv_copy.wait_recv()
+    key_low = ((key_own + dkv_in[0].astype(F32)) * SCORE_SCALE).astype(BF16)
+    value_grad = value_own + dkv_in[1].astype(F32)
+    value_low = value_grad.astype(BF16)
+    vec_s[0, V_BIAS : V_BIAS + 1, :heads_width] = column_sum(value_grad)
+    one_part = one_part + mm(key_low, weight_k, NT) + mm(value_low, weight_v, NT)
+    one_sum = sum_start(3, one_part)
+    for index, grad_low in enumerate((query_low, key_low, value_low)):
+        weight_grad = mm(normed_one, grad_low, TN).reshape(4, depth, heads_width)
+        for block in range(4):
+            attn_g[block, index] = weight_grad[block]
+    attn_copy = reduce_one(attn_g, attn_s1, attn_r1)
+    one_sum = sum_pass(3, one_sum)
+    attn_copy = reduce_two(attn_copy, attn_g, attn_r1, attn_s2, attn_r2)
+    down_copy = reduce_three(
+        down_copy, down_g, mlp_r1.at[1], mlp_r2.at[1], mlp_s3.at[1], mlp_r3.at[1]
+    )
+    up_copy = reduce_three(up_copy, up_g, mlp_r1.at[0], mlp_r2.at[0], mlp_s3.at[0], mlp_r3.at[0])
+    norm_one_grad = sum_end(3, one_sum)
+    vec_s[0, GAIN_ONE : GAIN_ONE + 1, :] = column_sum(norm_one_grad * unit_one)
+    vec_s[0, SHIFT_ONE : SHIFT_ONE + 1, :] = column_sum(norm_one_grad)
+    vec_copy = send(vec_s.at[0], vec_r.at[0], p1)
+    attn_copy = reduce_three(attn_copy, attn_g, attn_r1, attn_r2, attn_s3, attn_r3)
+    in_grad_ref[...] = mid_grad + normalize_back(
+        norm_one_grad, unit_one, inverse_one, row(GAIN_ONE)
+    )
+    vec_copy.wait_recv()
+    vec_s[1] = vec_s[0] + vec_r[0]
+    vec_copy = send(vec_s.at[1], vec_r.at[1], p2)
+    out_ref[...] = residual_mid + sum_end(1, out_sum) + row(DOWN_BIAS)
+    vec_copy.wait_recv()
+    vec_s[2] = vec_s[1] + vec_r[1]
+    vec_copy = send(vec_s.at[2], vec_r.at[2], pc)
+    reduce_end(down_copy, mlp_s3.at[1], mlp_r3.at[1], down_g_ref)
+    reduce_end(up_copy, mlp_s3.at[0], mlp_r3.at[0], up_g_ref)
+    reduce_end(attn_copy, attn_s3, attn_r3, attn_g_ref)
+    vec_copy.wait_recv()
+    vec_g_ref[...] = vec_s[2] + vec_r[2]
+    for copy in started:
+        copy.wait_send()
+
+
+def paired_body(
+    block_in, segment_ids, out_cotangent, attn_gain, attn_shift, qkv_weight, qv_bias, proj_weight,
+    proj_bias, mlp_gain, mlp_shift, up_weight, up_bias, down_weight, down_bias,
+):
+    shard = lax.axis_index("shard")
+    shards = lax.axis_size("shard")
+    _, tokens, width = block_in.shape
+    depth = qkv_weight.shape[0]
+    heads_width = qkv_weight.shape[2]
+    units = up_weight.shape[1]
+    head_count, head_piece = qv_bias.shape[1:]
+    up_rows, up_piece = up_bias.shape
+    wide = jnp.stack([attn_gain, attn_shift, proj_bias, mlp_gain, mlp_shift, down_bias]).astype(F32)
+
+    def placed(value):
+        axis = value.ndim - 1
+        size = value.shape[axis]
+        room = jnp.zeros(value.shape[:-1] + (size * shards,), F32)
+        return lax.dynamic_update_slice_in_dim(room, value, shard * size, axis)
+
+    wide = placed(wide)
+    up_row = placed(up_bias.astype(F32)).reshape(1, units)
+    qv_rows = placed(qv_bias.astype(F32)).reshape(2, heads_width)
+    qv_rows = jnp.pad(qv_rows, ((0, VEC_ROWS - 9), (0, width - heads_width)))
+    vec = jnp.concatenate([wide, up_row, qv_rows], axis=0)
+    attn_w = jnp.concatenate(
+        [jnp.transpose(qkv_weight, (1, 0, 2)), jnp.transpose(proj_weight)[None]], axis=0
+    )
+    segq = jnp.broadcast_to(segment_ids.reshape(tokens, 1), (tokens, tokens))
+    segk = jnp.broadcast_to(segment_ids.reshape(1, tokens), (8, tokens))
+    attn_shape = (4, depth, heads_width)
+    mlp_shape = (depth, units)
+    vmem = pltpu.VMEM
+    out_shapes = (
+        jax.ShapeDtypeStruct((tokens, width), F32),
+        jax.ShapeDtypeStruct((tokens, width), F32),
+        jax.ShapeDtypeStruct(attn_shape, F32),
+        jax.ShapeDtypeStruct(mlp_shape, F32),
+        jax.ShapeDtypeStruct(mlp_shape, F32),
+        jax.ShapeDtypeStruct((VEC_ROWS, width), F32),
+    )
+    scratch = [
+        vmem((4,) + attn_shape, BF16), vmem((4,) + mlp_shape, BF16), vmem((4,) + mlp_shape, BF16),
+        vmem((3, VEC_ROWS, width), F32), vmem((8, tokens), jnp.int32),
+        vmem((2, tokens, heads_width), BF16), vmem((2, tokens, heads_width), BF16),
+        vmem((2, tokens, heads_width), BF16), vmem((2, tokens, heads_width), BF16),
+        vmem((4, 4, tokens // 4, width), F32), vmem((4, 4, tokens // 4, width), BF16),
+        vmem((4, 3, tokens // 4, width), BF16), vmem((4, 4, tokens // 4, width), BF16),
+        vmem((4,) + attn_shape, F32), vmem((4,) + mlp_shape, F32), vmem((4,) + mlp_shape, F32),
+        vmem((2,) + attn_shape, BF16), vmem((2,) + attn_shape, BF16),
+        vmem(attn_shape, BF16), vmem(attn_shape, BF16), vmem(attn_shape, BF16), vmem(attn_shape, BF16),
+        vmem((2, 2) + mlp_shape, BF16), vmem((2, 2) + mlp_shape, BF16),
+        vmem((2,) + mlp_shape, BF16), vmem((2,) + mlp_shape, BF16),
+        vmem((2,) + mlp_shape, BF16), vmem((2,) + mlp_shape, BF16),
+        vmem((3, VEC_ROWS, width), F32), vmem((3, VEC_ROWS, width), F32),
+        pltpu.SemaphoreType.DMA((COPIES,)), pltpu.SemaphoreType.DMA((COPIES,)),
+    ]
+    whole = pl.BlockSpec(memory_space=pltpu.VMEM)
+    block_out, in_grad, attn_g, up_g, down_g, vec_g = pl.pallas_call(
+        block_kernel,
+        out_shape=out_shapes,
+        in_specs=[whole] * 8,
+        out_specs=(whole,) * 6,
+        scratch_shapes=scratch,
+        compiler_params=pltpu.CompilerParams(
+            collective_id=0, has_side_effects=True, vmem_limit_bytes=56 * 1024 * 1024
+        ),
+    )(
+        block_in[0], out_cotangent[0], segq, segk, attn_w, up_weight, jnp.transpose(down_weight), vec
+    )
+    mine = lax.dynamic_slice_in_dim(vec_g[:6], shard * depth, depth, 1)
+    up_b = lax.dynamic_slice_in_dim(
+        vec_g[UP_BIAS].reshape(up_rows, up_piece * shards), shard * up_piece, up_piece, 1
+    )
+    qv_b = lax.dynamic_slice_in_dim(
+        vec_g[Q_BIAS : V_BIAS + 1, :heads_width].reshape(2, head_count, head_piece * shards),
+        shard * head_piece, head_piece, 2,
+    )
+    return (
+        block_out[None], in_grad[None], mine[0], mine[1], jnp.transpose(attn_g[:3], (1, 0, 2)), qv_b,
+        jnp.transpose(attn_g[3]), mine[2], mine[3], mine[4], up_g, up_b, jnp.transpose(down_g), mine[5],
+    )
+
+
 def solution(mesh):
+    paired = mesh.shape["ctx"] == 2 and mesh.shape["shard"] == 4 and mesh.shape["tp"] == 4
     return jax.shard_map(
-        body,
+        paired_body if paired else body,
         mesh=mesh,
         in_specs=(
             P("shard", "ctx", None),

time: 386 us -> 111 us (0.29)
  waiting for transfers between devices: 202 us -> 0 us
  Pallas kernels: 0 us -> 86.9 us
  blocking collectives: 65.6 us -> 0 us
  matrix products: 25.4 us -> 0 us
  starting transfers between devices: 19.5 us -> 0 us
  between operations: 20.1 us -> 0.77 us
  other arithmetic: 19.7 us -> 2.14 us
  local copies, waits for them, and re-layouts: 32.3 us -> 20.8 us
    reduce_scatter x3 -> x0, waiting for transfers between devices: 102 us -> none  [the longest x1 35.7 us: body(): lax.psum_scatter(local_grads[10], 'shard', scatter_dimension=1, tiled=True)]
    pallas_call x0 -> x1, Pallas kernels: none -> 86.9 us  [paired_body(): pl.pallas_call(block_kernel, out_shape=out_shapes, in_specs=[whole] * 8,...]
    psum x4 -> x0, waiting for transfers between devices: 57.6 us -> none  [the longest x3 56.5 us: feature_sum(): return lax.psum(part_sum, 'tp')]
    all_gather x5 -> x0, blocking collectives: 34.5 us -> none  [the longest x1 13 us: body(): lax.all_gather(qkv_weight, 'shard', axis=0, tiled=True)]
    dot_general x24 -> x0, matrix products: 23.7 us -> none  [the longest x1 2.53 us: body(): jnp.dot(hidden, down_full, preferred_element_type=jnp.float32)]
    unnamed x15 -> x0, waiting for transfers between devices: 23.7 us -> none
    unnamed x2 -> x0, blocking collectives: 22.1 us -> none
    all_to_all x4 -> x0, starting transfers between devices: 14.6 us -> none  [the longest x1 4.21 us: body(): lax.all_to_all(block_in, 'ctx', split_axis=1, concat_axis=1, tiled=True)]
  transfers between devices with their start and end apart: 19 -> 0, of which waited for: 12 -> 0; matrix products, arithmetic and copies ran while one was open for 12% -> 0% of each run, Pallas kernels for 0% -> 0%
where the time goes in v1:
time: 111 us
  Pallas kernels  86.9 us (78%)
  local copies, waits for them, and re-layouts  20.8 us (19%)
  other arithmetic  2.14 us (2%)
    pallas_call x1, Pallas kernels, paired_body(): pl.pallas_call(block_kernel, out_shape=out_shapes, in_specs=[whole] * 8,...  86.9 us
    unnamed x20, local copies, waits for them, and re-layouts  7.01 us
    another operation x7, local copies, waits for them, and re-layouts, paired_body(): jnp.stack([attn_gain, attn_shift, proj_bias, mlp_gain, mlp_shift, down_bi...  4.02 us

profile of v1, /device:TPU:0, one launch (start us, length us, event | category | flops | bytes accessed | tf_op | source)
XLA Modules:
  0.0 110.6 jit_solution(17029159141574916756)
XLA Ops:
  0.7 0.7 stack.21
  1.4 0.7 stack.22
  2.0 0.7 stack.23
  2.7 0.7 stack.24
  3.3 0.7 stack.25
  4.0 0.7 stack.26
  4.7 1.2 %broadcast_in_dim.32.segk_ref = s32[8,128]{1,0:T(8,128)} broadcast(s32[128]{0:T(128)} %bitcast.40), dimensions={1} | broadcast | bytes 4608 | tf_op jit(solution)/shard_map/broadcast_in_dim | solution.py:736
  5.9 0.7 copy.34
  6.6 0.7 convert_element_type.12
  7.5 0.1 dynamic_update_slice.10
  7.7 0.3 dynamic_update_slice.9
  8.0 0.6 select_maximum_fusion.vec_ref
  8.6 1.4 %broadcast_in_dim.31.segq_ref = s32[128,128]{1,0:T(8,128)} broadcast(s32[128]{0:T(128)} %bitcast.41), dimensions={0} | broadcast | bytes 66048 | tf_op jit(solution)/shard_map/broadcast_in_dim | solution.py:735
  10.0 1.0 copy.33
  11.0 0.8 pad_maximum_fusion.attn_w
  11.8 86.9 %shard_map.254 = (f32[128,768]{1,0:T(8,128)}, f32[128,768]{1,0:T(8,128)}, f32[4,192,192]{2,1,0:T(8,128)}, f32[192,768]{1,0:T(8,128)}, f32[192,768]{1,0:T(8,128)}, /*index=5*/f32[16,768]{1,0:T(8,128)}) custom-call(bf16[128,768]{1,0:T(8,128)(2,1)} %bitcast.35, bf16[128,768]{1,0:T(8,128)(2,1)} %bitcast.36, s32[128,128]{1,0:T(8,128)} %broadcast_in_dim.31.segq_ref, ...), custom_call_target="tpu_custom_call" | custom-call | tf_op jit(solution)/shard_map/pallas_call | solution.py:765
  98.7 0.8 slice.37
  99.6 0.6 copy.35
  100.2 0.8 slice_reduce_fusion
  101.0 0.7 fusion
  101.7 0.7 constant_dynamic-slice_fusion.1
  102.3 0.9 slice_bitcast_fusion.1
  103.3 1.9 %slice_bitcast_fusion = f32[192,3,192]{2,0,1:T(8,128)} fusion(f32[4,192,192]{2,1,0:T(8,128)} %get-tuple-element.23), kind=kLoop, calls=%fused_computation | loop fusion | bytes 884736 | tf_op jit(solution)/shard_map/transpose | solution.py:786
  105.2 0.8 copy.36
  106.0 0.2 copy-done.3
  106.2 0.7 copy.47
  107.0 0.4 copy-done.2
  107.3 0.7 copy.48
  108.1 0.5 copy-done.1
  108.5 0.8 copy.49
  109.4 0.5 copy-done
  109.8 0.8 copy.50
  (19 shorter events, 0.4 us)
Async XLA Ops:
  0.6 10.3 %copy-start.4 = (bf16[192,3,192]{2,0,1:T(8,128)(2,1)S(1)}, bf16[192,3,192]{2,0,1:T(8,128)(2,1)}, u32[]{:S(2)}) copy-start(bf16[192,3,192]{2,0,1:T(8,128)(2,1)} %param.20) | copy-start | bytes 663556
  98.7 2.3 %copy-start.5 = (f32[16,768]{1,0:T(8,128)S(1)}, f32[16,768]{1,0:T(8,128)}, u32[]{:S(2)}) copy-start(f32[16,768]{1,0:T(8,128)} %get-tuple-element.22) | copy-start | bytes 147460
  105.2 1.0 copy-start.3
  106.2 1.1 %copy-start.2 = (f32[128,768]{1,0:T(8,128)S(1)}, f32[128,768]{1,0:T(8,128)}, u32[]{:S(2)}) copy-start(f32[128,768]{1,0:T(8,128)} %get-tuple-element.21) | copy-start | bytes 1179652
  107.3 1.2 %copy-start.1 = (f32[192,768]{1,0:T(8,128)S(1)}, f32[192,768]{1,0:T(8,128)}, u32[]{:S(2)}) copy-start(f32[192,768]{1,0:T(8,128)} %get-tuple-element.84) | copy-start | bytes 1769476
  108.5 1.3 %copy-start = (f32[192,768]{1,0:T(8,128)S(1)}, f32[192,768]{1,0:T(8,128)}, u32[]{:S(2)}) copy-start(f32[192,768]{1,0:T(8,128)} %get-tuple-element.25) | copy-start | bytes 1769476

commit v2 on v1

--- a/solution.py
+++ b/solution.py
@@ -408,9 +408,10 @@
 MESH = pl.DeviceIdType.MESH
 F32 = jnp.float32
 BF16 = jnp.bfloat16
-GAIN_ONE, SHIFT_ONE, PROJ_BIAS, GAIN_TWO, SHIFT_TWO, DOWN_BIAS, UP_BIAS, Q_BIAS, V_BIAS = range(9)
+GAIN_ONE, SHIFT_ONE, PROJ_BIAS, GAIN_TWO, SHIFT_TWO, DOWN_BIAS, Q_BIAS, V_BIAS, UP_BIAS = range(9)
 VEC_ROWS = 16
 COPIES = 64
+VMEM_LIMIT = 56 * 1024 * 1024
 
 
 def mm(left, right, dims=((1,), (0,))):
@@ -421,13 +422,73 @@
 TN = ((0,), (0,))
 
 
+def identity(size):
+    at_row = lax.broadcasted_iota(jnp.int32, (size, size), 0)
+    at_column = lax.broadcasted_iota(jnp.int32, (size, size), 1)
+    return jnp.where(at_row == at_column, 1.0, 0.0).astype(BF16)
+
+
+def pack_vectors(vec_ref, wide_ref, qv_ref, up_b_ref, shard):
+    width = vec_ref.shape[1]
+    depth = width // 4
+    heads, _, piece = qv_ref.shape
+    up_rows, up_piece = up_b_ref.shape
+    vec_ref[...] = jnp.zeros_like(vec_ref)
+    vec_ref[0:8, :depth] = wide_ref[...]
+    wide = vec_ref[0:8, :]
+    wide = pltpu.roll(wide, shard * depth, 1)
+    span = 128 * ((4 * heads * piece + 127) // 128)
+    qv_sum = jnp.zeros((8, span), F32)
+    for head in range(heads):
+        vec_ref[8:16, :] = jnp.zeros((8, width), F32)
+        vec_ref[8:10, :piece] = qv_ref[head].astype(F32)
+        qv_sum = qv_sum + pltpu.roll(vec_ref[8:16, :span], head * 4 * piece + shard * piece, 1)
+    vec_ref[8:16, :] = jnp.zeros((8, width), F32)
+    vec_ref[8 : 8 + up_rows, :up_piece] = up_b_ref[...].astype(F32)
+    up_part = pltpu.roll(vec_ref[8:16, :128], shard * up_piece, 1)
+    vec_ref[0:8, :] = wide
+    vec_ref[Q_BIAS : Q_BIAS + 2, :span] = qv_sum[0:2]
+    vec_ref[8:16, :128] = up_part
+
+
+def finish_kernel(
+    out_in, in_grad_in, attn_s3, attn_r3, mlp_s3, mlp_r3, vec_ref,
+    out_ref, in_grad_ref, qkv_g_ref, proj_g_ref, up_g_ref, down_g_ref,
+    gain_one_ref, shift_one_ref, proj_b_ref, gain_two_ref, shift_two_ref, down_b_ref, qv_g_ref, up_b_ref,
+):
+    shard = lax.axis_index("shard")
+    width = vec_ref.shape[1]
+    depth = width // 4
+    heads, _, piece = qv_g_ref.shape
+    up_rows, up_piece = up_b_ref.shape
+    out_ref[...] = out_in[...]
+    in_grad_ref[...] = in_grad_in[...]
+    qkv_g_ref[...] = attn_s3[0:3].astype(F32) + attn_r3[0:3].astype(F32)
+    unit = identity(depth)
+    proj_g_ref[...] = mm(attn_s3[3], unit, TN) + mm(attn_r3[3], unit, TN)
+    up_g_ref[...] = mlp_s3[0].astype(F32) + mlp_r3[0].astype(F32)
+    down_g_ref[...] = mlp_s3[1].astype(F32) + mlp_r3[1].astype(F32)
+    wide = pltpu.roll(vec_ref[0:8, :], lax.rem(width - shard * depth, width), 1)
+    wide_refs = (gain_one_ref, shift_one_ref, proj_b_ref, gain_two_ref, shift_two_ref, down_b_ref)
+    for index, ref in enumerate(wide_refs):
+        ref[...] = wide[index : index + 1, :depth]
+    span = 128 * ((4 * heads * piece + 127) // 128)
+    for head in range(heads):
+        turned = pltpu.roll(
+            vec_ref[0:8, :span], lax.rem(span - head * 4 * piece - shard * piece, span), 1
+        )
+        qv_g_ref[head] = turned[Q_BIAS : Q_BIAS + 2, :piece]
+    turned = pltpu.roll(vec_ref[8:16, :128], lax.rem(128 - shard * up_piece, 128), 1)
+    up_b_ref[...] = turned[:up_rows, :up_piece]
+
+
 def block_kernel(
-    x_ref, cot_ref, segq_ref, segk_ref, attn_w, up_w, down_w, vec_ref,
-    out_ref, in_grad_ref, attn_g_ref, up_g_ref, down_g_ref, vec_g_ref,
-    attn_f, up_f, down_f, vec_in, segk_in, kv, kv_in, dkv, dkv_in,
+    x_ref, cot_ref, seg_ref, qkv_w, proj_w, up_w, down_w, wide_ref, qv_ref, up_b_ref,
+    out_ref, in_grad_ref, attn_s3, attn_r3, mlp_s3, mlp_r3, vec_g_ref,
+    qkv_f, proj_t, proj_f, up_f, down_f, vec_ref, vec_in, segk, segk_in, kv, kv_in, dkv, dkv_in,
     part, ar_send, ar_recv, ar_all,
-    attn_g, up_g, down_g, attn_s1, attn_r1, attn_s2, attn_r2, attn_s3, attn_r3,
-    mlp_s1, mlp_r1, mlp_s2, mlp_r2, mlp_s3, mlp_r3,
+    attn_g, up_g, down_g, attn_s1, attn_r1, attn_s2, attn_r2,
+    mlp_s1, mlp_r1, mlp_s2, mlp_r2,
     vec_s, vec_r, send_sem, recv_sem,
 ):
     shard = lax.axis_index("shard")
@@ -443,7 +504,7 @@
     tps = [lax.rem(tp + step, 4) for step in (1, 2, 3)]
     tokens, width = x_ref.shape
     depth = up_w.shape[0]
-    heads_width = attn_w.shape[2]
+    heads_width = qkv_w.shape[2]
     head_count = heads_width // 64
 
     barrier = pltpu.get_barrier_semaphore()
@@ -469,6 +530,9 @@
         inverse = lax.rsqrt(jnp.mean(shifted * shifted, axis=-1, keepdims=True) + EPSILON)
         return shifted * inverse, inverse
 
+    pack_vectors(vec_ref, wide_ref, qv_ref, up_b_ref, shard)
+    segk[...] = jnp.broadcast_to(seg_ref[...], segk.shape)
+    proj_t[...] = mm(proj_w[...], identity(heads_width), TN).astype(BF16)
     pl.semaphore_wait(barrier, len(peers))
 
     def gather_start(local, full):
@@ -480,10 +544,11 @@
         far.wait_recv()
         return send(full.at[s2], full.at[s2], p1)
 
-    attn_far, attn_near = gather_start(attn_w, attn_f)
+    qkv_far, qkv_near = gather_start(qkv_w, qkv_f)
     vec_copies = [send(vec_ref, vec_in.at[i], p) for i, p in enumerate((p1, p2, p3))]
-    seg_copy = send(segk_ref, segk_in, pc)
-    attn_f[shard] = attn_w[...]
+    seg_copy = send(segk, segk_in, pc)
+    qkv_f[shard] = qkv_w[...]
+    proj_f[shard] = proj_t[...]
     up_f[shard] = up_w[...]
     down_f[shard] = down_w[...]
     residual_in = x_ref[...].astype(F32)
@@ -492,17 +557,22 @@
         copy.wait_recv()
     vec = vec_ref[...] + vec_in[0] + vec_in[1] + vec_in[2]
 
+    up_bias = jnp.concatenate(
+        [vec[UP_BIAS + r : UP_BIAS + r + 1, :128] for r in range(up_b_ref.shape[0])], axis=1
+    )
+
     def row(index, size=width):
         return vec[index : index + 1, :size]
 
     normed_one = (unit_one * row(GAIN_ONE) + row(SHIFT_ONE)).astype(BF16)
-    attn_pass = gather_pass(attn_f, attn_far)
+    qkv_pass = gather_pass(qkv_f, qkv_far)
+    proj_far, proj_near = gather_start(proj_t, proj_f)
     up_far, up_near = gather_start(up_w, up_f)
     down_far, down_near = gather_start(down_w, down_f)
-    attn_near.wait_recv()
-    attn_pass.wait_recv()
-    weight_q, weight_k, weight_v, weight_p = (
-        attn_f[:, index].reshape(4 * depth, heads_width) for index in range(4)
+    qkv_near.wait_recv()
+    qkv_pass.wait_recv()
+    weight_q, weight_k, weight_v = (
+        qkv_f[:, index].reshape(4 * depth, heads_width) for index in range(3)
     )
     keys = mm(normed_one, weight_k).astype(BF16)
     values = (mm(normed_one, weight_v) + row(V_BIAS, heads_width)).astype(BF16)
@@ -520,14 +590,15 @@
     seg_copy.wait_recv()
     query_at = lax.broadcasted_iota(jnp.int32, (tokens, tokens), 0)
     key_at = lax.broadcasted_iota(jnp.int32, (tokens, tokens), 1)
-    segq = segq_ref[...]
-    allow_own = (key_at <= query_at) & (segq == segk_ref[0:1, :])
+    segq = jnp.transpose(jnp.broadcast_to(seg_ref[...].astype(F32), (tokens, tokens))).astype(jnp.int32)
+    allow_own = (key_at <= query_at) & (segq == segk[0:1, :])
     allow_other = (segq == segk_in[0:1, :]) & (key_at + tokens * (1 - ctx) <= query_at + tokens * ctx)
     query_of = [pick(queries, index) for index in range(head_count)]
     score_own = [
         jnp.where(allow_own, mm(query_of[i], keys, NT) * SCORE_SCALE, NEGATIVE)
         for i in range(head_count)
     ]
+    proj_pass = gather_pass(proj_f, proj_far)
     kv_copy.wait_recv()
     keys_other = kv_in[0]
     values_other = kv_in[1]
@@ -570,6 +641,9 @@
             copy.wait_recv()
         return ar_all[phase].reshape(tokens, width).astype(F32)
 
+    proj_near.wait_recv()
+    proj_pass.wait_recv()
+    weight_p = proj_f[...].reshape(4 * depth, heads_width)
     mid_sum = sum_start(0, mm(mixed, weight_p, NT))
     up_pass = gather_pass(up_f, up_far)
     mid_sum = sum_pass(0, mid_sum)
@@ -580,7 +654,7 @@
     up_near.wait_recv()
     up_pass.wait_recv()
     up_full = up_f[...].reshape(4 * depth, up_f.shape[2])
-    pre_gelu = mm(normed_two, up_full) + row(UP_BIAS)
+    pre_gelu = mm(normed_two, up_full) + up_bias
     tangent = jnp.tanh(GELU_ROOT * (pre_gelu + GELU_CUBIC * pre_gelu * pre_gelu * pre_gelu))
     hidden = (0.5 * pre_gelu * (1.0 + tangent)).astype(BF16)
     slope = 0.5 * (1.0 + tangent) + 0.5 * pre_gelu * (1.0 - tangent * tangent) * GELU_ROOT * (
@@ -600,7 +674,9 @@
         return jnp.sum(value, axis=0, keepdims=True)
 
     vec_s[0] = jnp.zeros((VEC_ROWS, width), F32)
-    vec_s[0, UP_BIAS : UP_BIAS + 1, :] = column_sum(pre_grad)
+    up_bias_grad = column_sum(pre_grad)
+    for r in range(up_b_ref.shape[0]):
+        vec_s[0, UP_BIAS + r : UP_BIAS + r + 1, :128] = up_bias_grad[:, 128 * r : 128 * (r + 1)]
     vec_s[0, DOWN_BIAS : DOWN_BIAS + 1, :] = column_sum(cot_high)
 
     def reduce_one(grads, s1_buf, r1_buf):
@@ -619,10 +695,6 @@
             grads[shard] + r1_buf[high].astype(F32) + r2_buf[...].astype(F32)
         ).astype(BF16)
         return send(s3_buf, r3_buf, pc)
-
-    def reduce_end(copy, s3_buf, r3_buf, result):
-        copy.wait_recv()
-        result[...] = s3_buf[...].astype(F32) + r3_buf[...].astype(F32)
 
     down_g[...] = mm(cot_low, hidden, TN).reshape(down_g.shape)
     down_copy = reduce_one(down_g, mlp_s1.at[1], mlp_r1.at[1])
@@ -695,9 +767,9 @@
     vec_copy.wait_recv()
     vec_s[2] = vec_s[1] + vec_r[1]
     vec_copy = send(vec_s.at[2], vec_r.at[2], pc)
-    reduce_end(down_copy, mlp_s3.at[1], mlp_r3.at[1], down_g_ref)
-    reduce_end(up_copy, mlp_s3.at[0], mlp_r3.at[0], up_g_ref)
-    reduce_end(attn_copy, attn_s3, attn_r3, attn_g_ref)
+    down_copy.wait_recv()
+    up_copy.wait_recv()
+    attn_copy.wait_recv()
     vec_copy.wait_recv()
     vec_g_ref[...] = vec_s[2] + vec_r[2]
     for copy in started:
@@ -708,83 +780,83 @@
     block_in, segment_ids, out_cotangent, attn_gain, attn_shift, qkv_weight, qv_bias, proj_weight,
     proj_bias, mlp_gain, mlp_shift, up_weight, up_bias, down_weight, down_bias,
 ):
-    shard = lax.axis_index("shard")
-    shards = lax.axis_size("shard")
     _, tokens, width = block_in.shape
     depth = qkv_weight.shape[0]
     heads_width = qkv_weight.shape[2]
     units = up_weight.shape[1]
     head_count, head_piece = qv_bias.shape[1:]
-    up_rows, up_piece = up_bias.shape
-    wide = jnp.stack([attn_gain, attn_shift, proj_bias, mlp_gain, mlp_shift, down_bias]).astype(F32)
-
-    def placed(value):
-        axis = value.ndim - 1
-        size = value.shape[axis]
-        room = jnp.zeros(value.shape[:-1] + (size * shards,), F32)
-        return lax.dynamic_update_slice_in_dim(room, value, shard * size, axis)
-
-    wide = placed(wide)
-    up_row = placed(up_bias.astype(F32)).reshape(1, units)
-    qv_rows = placed(qv_bias.astype(F32)).reshape(2, heads_width)
-    qv_rows = jnp.pad(qv_rows, ((0, VEC_ROWS - 9), (0, width - heads_width)))
-    vec = jnp.concatenate([wide, up_row, qv_rows], axis=0)
-    attn_w = jnp.concatenate(
-        [jnp.transpose(qkv_weight, (1, 0, 2)), jnp.transpose(proj_weight)[None]], axis=0
-    )
-    segq = jnp.broadcast_to(segment_ids.reshape(tokens, 1), (tokens, tokens))
-    segk = jnp.broadcast_to(segment_ids.reshape(1, tokens), (8, tokens))
+    at_row = lax.broadcasted_iota(jnp.int32, (8, depth), 0)
+    wide = jnp.zeros((8, depth), F32)
+    vectors = (attn_gain, attn_shift, proj_bias, mlp_gain, mlp_shift, down_bias)
+    for index, vector in enumerate(vectors):
+        wide = jnp.where(at_row == index, vector.astype(F32)[None, :], wide)
     attn_shape = (4, depth, heads_width)
     mlp_shape = (depth, units)
     vmem = pltpu.VMEM
-    out_shapes = (
-        jax.ShapeDtypeStruct((tokens, width), F32),
-        jax.ShapeDtypeStruct((tokens, width), F32),
-        jax.ShapeDtypeStruct(attn_shape, F32),
-        jax.ShapeDtypeStruct(mlp_shape, F32),
-        jax.ShapeDtypeStruct(mlp_shape, F32),
-        jax.ShapeDtypeStruct((VEC_ROWS, width), F32),
-    )
+    shaped = jax.ShapeDtypeStruct
+    middle_shapes = (
+        shaped((tokens, width), F32),
+        shaped((tokens, width), F32),
+        shaped(attn_shape, BF16),
+        shaped(attn_shape, BF16),
+        shaped((2,) + mlp_shape, BF16),
+        shaped((2,) + mlp_shape, BF16),
+        shaped((VEC_ROWS, width), F32),
+    )
+    proj_shape = (depth, heads_width)
+    qkv_shape = (3, depth, heads_width)
     scratch = [
-        vmem((4,) + attn_shape, BF16), vmem((4,) + mlp_shape, BF16), vmem((4,) + mlp_shape, BF16),
-        vmem((3, VEC_ROWS, width), F32), vmem((8, tokens), jnp.int32),
+        vmem((4,) + qkv_shape, BF16), vmem(proj_shape, BF16), vmem((4,) + proj_shape, BF16),
+        vmem((4,) + mlp_shape, BF16), vmem((4,) + mlp_shape, BF16),
+        vmem((VEC_ROWS, width), F32), vmem((3, VEC_ROWS, width), F32),
+        vmem((8, tokens), jnp.int32), vmem((8, tokens), jnp.int32),
         vmem((2, tokens, heads_width), BF16), vmem((2, tokens, heads_width), BF16),
         vmem((2, tokens, heads_width), BF16), vmem((2, tokens, heads_width), BF16),
         vmem((4, 4, tokens // 4, width), F32), vmem((4, 4, tokens // 4, width), BF16),
         vmem((4, 3, tokens // 4, width), BF16), vmem((4, 4, tokens // 4, width), BF16),
         vmem((4,) + attn_shape, F32), vmem((4,) + mlp_shape, F32), vmem((4,) + mlp_shape, F32),
         vmem((2,) + attn_shape, BF16), vmem((2,) + attn_shape, BF16),
-        vmem(attn_shape, BF16), vmem(attn_shape, BF16), vmem(attn_shape, BF16), vmem(attn_shape, BF16),
+        vmem(attn_shape, BF16), vmem(attn_shape, BF16),
         vmem((2, 2) + mlp_shape, BF16), vmem((2, 2) + mlp_shape, BF16),
-        vmem((2,) + mlp_shape, BF16), vmem((2,) + mlp_shape, BF16),
         vmem((2,) + mlp_shape, BF16), vmem((2,) + mlp_shape, BF16),
         vmem((3, VEC_ROWS, width), F32), vmem((3, VEC_ROWS, width), F32),
         pltpu.SemaphoreType.DMA((COPIES,)), pltpu.SemaphoreType.DMA((COPIES,)),
     ]
     whole = pl.BlockSpec(memory_space=pltpu.VMEM)
-    block_out, in_grad, attn_g, up_g, down_g, vec_g = pl.pallas_call(
+    middle = pl.pallas_call(
         block_kernel,
-        out_shape=out_shapes,
-        in_specs=[whole] * 8,
-        out_specs=(whole,) * 6,
+        out_shape=middle_shapes,
+        in_specs=[whole] * 10,
+        out_specs=(whole,) * 7,
         scratch_shapes=scratch,
         compiler_params=pltpu.CompilerParams(
-            collective_id=0, has_side_effects=True, vmem_limit_bytes=56 * 1024 * 1024
+            collective_id=0, has_side_effects=True, vmem_limit_bytes=VMEM_LIMIT
         ),
     )(
-        block_in[0], out_cotangent[0], segq, segk, attn_w, up_weight, jnp.transpose(down_weight), vec
-    )
-    mine = lax.dynamic_slice_in_dim(vec_g[:6], shard * depth, depth, 1)
-    up_b = lax.dynamic_slice_in_dim(
-        vec_g[UP_BIAS].reshape(up_rows, up_piece * shards), shard * up_piece, up_piece, 1
-    )
-    qv_b = lax.dynamic_slice_in_dim(
-        vec_g[Q_BIAS : V_BIAS + 1, :heads_width].reshape(2, head_count, head_piece * shards),
-        shard * head_piece, head_piece, 2,
-    )
+        block_in[0], out_cotangent[0], segment_ids, jnp.transpose(qkv_weight, (1, 0, 2)), proj_weight,
+        up_weight, jnp.transpose(down_weight), wide, jnp.transpose(qv_bias, (1, 0, 2)), up_bias,
+    )
+    one_row = shaped((1, depth), F32)
+    result_shapes = (
+        shaped((tokens, width), F32), shaped((tokens, width), F32), shaped(qkv_shape, F32),
+        shaped((heads_width, depth), F32), shaped(mlp_shape, F32), shaped(mlp_shape, F32),
+        one_row, one_row, one_row, one_row, one_row, one_row,
+        shaped((head_count, 2, head_piece), F32), shaped(up_bias.shape, F32),
+    )
+    (
+        block_out, in_grad, qkv_g, proj_g, up_g, down_g,
+        gain_one, shift_one, proj_b, gain_two, shift_two, down_b, qv_b, up_b,
+    ) = pl.pallas_call(
+        finish_kernel,
+        out_shape=result_shapes,
+        in_specs=[whole] * 7,
+        out_specs=(whole,) * 14,
+        compiler_params=pltpu.CompilerParams(vmem_limit_bytes=16 * 1024 * 1024),
+    )(*middle)
     return (
-        block_out[None], in_grad[None], mine[0], mine[1], jnp.transpose(attn_g[:3], (1, 0, 2)), qv_b,
-        jnp.transpose(attn_g[3]), mine[2], mine[3], mine[4], up_g, up_b, jnp.transpose(down_g), mine[5],
+        block_out[None], in_grad[None], gain_one[0], shift_one[0], jnp.transpose(qkv_g, (1, 0, 2)),
+        jnp.transpose(qv_b, (1, 0, 2)), proj_g, proj_b[0], gain_two[0], shift_two[0], up_g, up_b,
+        jnp.transpose(down_g), down_b[0],
     )
 
 

time: 111 us -> 99.3 us (0.89)
  local copies, waits for them, and re-layouts: 20.8 us -> 10.8 us
  other arithmetic: 2.14 us -> 0.71 us
    another operation x7 -> x0, local copies, waits for them, and re-layouts: 4.02 us -> none  [paired_body(): jnp.stack([attn_gain, attn_shift, proj_bias, mlp_gain, mlp_shift, down_bi...]
    unnamed x20 -> x26, local copies, waits for them, and re-layouts: 7.01 us -> 10.8 us
    transpose x2 -> x0, local copies, waits for them, and re-layouts: 2.86 us -> none  [the longest x1 1.92 us: paired_body(): jnp.transpose(attn_g[:3], (1, 0, 2))]
    broadcast_in_dim x5 -> x0, local copies, waits for them, and re-layouts: 2.62 us -> none  [the longest x1 1.37 us: paired_body(): segq = jnp.broadcast_to(segment_ids.reshape(tokens, 1), (tokens, tokens))]
    slice x4 -> x0, local copies, waits for them, and re-layouts: 2.21 us -> none  [the longest x1 0.79 us: paired_body(): vec_g[Q_BIAS:V_BIAS + 1, :heads_width]]
    concatenate x2 -> x0, other arithmetic: 1.45 us -> none  [the longest x1 0.81 us: paired_body(): jnp.concatenate([jnp.transpose(qkv_weight, (1, 0, 2)), jnp.transpose(proj...]
    pallas_call x1 -> x2, Pallas kernels: 86.9 us -> 86.6 us  [the longest x1 84.8 us: paired_body(): pl.pallas_call(block_kernel, out_shape=middle_shapes, in_specs=[whole] *...]
where the time goes in v2:
time: 99.3 us; the launch traced here: 98.8 us
  Pallas kernels  86.6 us (87%)
  local copies, waits for them, and re-layouts  10.8 us (11%)
    pallas_call x1, Pallas kernels, paired_body(): pl.pallas_call(block_kernel, out_shape=middle_shapes, in_specs=[whole] *...  84.8 us
    unnamed x26, local copies, waits for them, and re-layouts  10.8 us

profile of v2, /device:TPU:0, one launch (start us, length us, event | category | flops | bytes accessed | tf_op | source)
XLA Modules:
  0.0 98.8 jit_solution(14695415092943558624)
XLA Ops:
  0.6 0.0 copy-start.7
  0.7 0.6 copy-done.7
  1.3 0.0 copy-start.8
  1.3 0.7 copy-done.8
  2.0 0.0 copy-start.9
  2.0 0.7 copy-done.9
  2.6 0.0 copy-start.10
  2.6 0.7 copy-done.10
  3.3 0.0 copy-start.11
  3.3 0.7 copy-done.11
  3.9 0.0 copy-start.12
  3.9 0.7 copy-done.12
  4.6 0.7 select_select_fusion.wide_ref
  5.3 84.8 %shard_map.254 = (f32[128,768]{1,0:T(8,128)}, f32[128,768]{1,0:T(8,128)}, bf16[4,192,192]{2,1,0:T(8,128)(2,1)}, bf16[4,192,192]{2,1,0:T(8,128)(2,1)}, bf16[2,192...) custom-call(bf16[128,768]{1,0:T(8,128)(2,1)} %bitcast.18, bf16[128,768]{1,0:T(8,128)(2,1)} %bitcast.19, ...), custom_call_target="tpu_custom_call" | custom-call | tf_op jit(solution)/shard_map/pallas_call | solution.py:826
  90.1 0.0 copy-start
  90.1 1.1 %copy-done = bf16[2,192,768]{2,1,0:T(8,128)(2,1)S(1)} copy-done((bf16[2,192,768]{2,1,0:T(8,128)(2,1)S(1)}, bf16[2,192,768]{2,1,0:T(8,128)(2,1)}, u32[]{:S(2)}) %copy-start) | copy-done | bytes 589848
  91.2 0.0 copy-start.1
  91.2 1.1 %copy-done.1 = bf16[2,192,768]{2,1,0:T(8,128)(2,1)S(1)} copy-done((bf16[2,192,768]{2,1,0:T(8,128)(2,1)S(1)}, bf16[2,192,768]{2,1,0:T(8,128)(2,1)}, u32[]{:S(2)}) %copy-start.1) | copy-done | bytes 589848
  92.3 0.0 copy-start.2
  92.3 1.0 %copy-done.2 = f32[128,768]{1,0:T(8,128)S(1)} copy-done((f32[128,768]{1,0:T(8,128)S(1)}, f32[128,768]{1,0:T(8,128)}, u32[]{:S(2)}) %copy-start.2) | copy-done | bytes 393240
  93.3 0.0 copy-start.3
  93.3 1.0 %copy-done.3 = f32[128,768]{1,0:T(8,128)S(1)} copy-done((f32[128,768]{1,0:T(8,128)S(1)}, f32[128,768]{1,0:T(8,128)}, u32[]{:S(2)}) %copy-start.3) | copy-done | bytes 393240
  94.3 0.0 copy-start.4
  94.3 1.0 %copy-done.4 = bf16[4,192,192]{2,1,0:T(8,128)(2,1)S(1)} copy-done((bf16[4,192,192]{2,1,0:T(8,128)(2,1)S(1)}, bf16[4,192,192]{2,1,0:T(8,128)(2,1)}, u32[]{:S(2)}) %copy-start.4) | copy-done | bytes 294936
  95.3 0.0 copy-start.5
  95.3 1.0 %copy-done.5 = bf16[4,192,192]{2,1,0:T(8,128)(2,1)S(1)} copy-done((bf16[4,192,192]{2,1,0:T(8,128)(2,1)S(1)}, bf16[4,192,192]{2,1,0:T(8,128)(2,1)}, u32[]{:S(2)}) %copy-start.5) | copy-done | bytes 294936
  96.2 0.0 copy-start.6
  96.2 0.8 copy-done.6
  97.0 1.7 %shard_map.255 = (f32[128,768]{1,0:T(8,128)}, f32[128,768]{1,0:T(8,128)}, f32[3,192,192]{2,1,0:T(8,128)}, f32[192,192]{1,0:T(8,128)}, f32[192,768]{1,0:T(8,128)}...) custom-call(f32[128,768]{1,0:T(8,128)S(1)} %copy-done.2, ...), custom_call_target="tpu_custom_call" | custom-call | tf_op jit(solution)/shard_map/pallas_call | solution.py:849
  (9 shorter events, 0.0 us)
Async XLA Ops:
  0.6 0.7 copy-start.7
  1.3 0.7 copy-start.8
  2.0 0.7 copy-start.9
  2.6 0.7 copy-start.10
  3.3 0.7 copy-start.11
  3.9 0.7 copy-start.12
  90.1 1.1 %copy-start = (bf16[2,192,768]{2,1,0:T(8,128)(2,1)S(1)}, bf16[2,192,768]{2,1,0:T(8,128)(2,1)}, u32[]{:S(2)}) copy-start(bf16[2,192,768]{2,1,0:T(8,128)(2,1)} %get-tuple-element.39.mlp_s3) | copy-start | bytes 1769476
  91.2 1.1 %copy-start.1 = (bf16[2,192,768]{2,1,0:T(8,128)(2,1)S(1)}, bf16[2,192,768]{2,1,0:T(8,128)(2,1)}, u32[]{:S(2)}) copy-start(bf16[2,192,768]{2,1,0:T(8,128)(2,1)} %get-tuple-element.40.mlp_r3) | copy-start | bytes 1769476
  92.3 1.0 %copy-start.2 = (f32[128,768]{1,0:T(8,128)S(1)}, f32[128,768]{1,0:T(8,128)}, u32[]{:S(2)}) copy-start(f32[128,768]{1,0:T(8,128)} %get-tuple-element.35.out_in) | copy-start | bytes 1179652
  93.3 1.0 %copy-start.3 = (f32[128,768]{1,0:T(8,128)S(1)}, f32[128,768]{1,0:T(8,128)}, u32[]{:S(2)}) copy-start(f32[128,768]{1,0:T(8,128)} %get-tuple-element.36.in_grad_in) | copy-start | bytes 1179652
  94.3 1.0 %copy-start.4 = (bf16[4,192,192]{2,1,0:T(8,128)(2,1)S(1)}, bf16[4,192,192]{2,1,0:T(8,128)(2,1)}, u32[]{:S(2)}) copy-start(bf16[4,192,192]{2,1,0:T(8,128)(2,1)} %get-tuple-element.37.attn_s3) | copy-start | bytes 884740
  95.3 1.0 %copy-start.5 = (bf16[4,192,192]{2,1,0:T(8,128)(2,1)S(1)}, bf16[4,192,192]{2,1,0:T(8,128)(2,1)}, u32[]{:S(2)}) copy-start(bf16[4,192,192]{2,1,0:T(8,128)(2,1)} %get-tuple-element.38.attn_r3) | copy-start | bytes 884740
  96.2 0.8 copy-start.6

commit v3 on v2

--- a/solution.py
+++ b/solution.py
@@ -452,17 +452,19 @@
 
 
 def finish_kernel(
-    out_in, in_grad_in, attn_s3, attn_r3, mlp_s3, mlp_r3, vec_ref,
+    sums_ref, attn_pair, mlp_pair,
     out_ref, in_grad_ref, qkv_g_ref, proj_g_ref, up_g_ref, down_g_ref,
     gain_one_ref, shift_one_ref, proj_b_ref, gain_two_ref, shift_two_ref, down_b_ref, qv_g_ref, up_b_ref,
 ):
+    attn_s3, attn_r3, mlp_s3, mlp_r3 = attn_pair.at[0], attn_pair.at[1], mlp_pair.at[0], mlp_pair.at[1]
     shard = lax.axis_index("shard")
-    width = vec_ref.shape[1]
+    tokens, width = out_ref.shape
+    vec_ref = sums_ref.at[2 * tokens : 2 * tokens + VEC_ROWS]
     depth = width // 4
     heads, _, piece = qv_g_ref.shape
     up_rows, up_piece = up_b_ref.shape
-    out_ref[...] = out_in[...]
-    in_grad_ref[...] = in_grad_in[...]
+    out_ref[...] = sums_ref[0:tokens]
+    in_grad_ref[...] = sums_ref[tokens : 2 * tokens]
     qkv_g_ref[...] = attn_s3[0:3].astype(F32) + attn_r3[0:3].astype(F32)
     unit = identity(depth)
     proj_g_ref[...] = mm(attn_s3[3], unit, TN) + mm(attn_r3[3], unit, TN)
@@ -484,13 +486,14 @@
 
 def block_kernel(
     x_ref, cot_ref, seg_ref, qkv_w, proj_w, up_w, down_w, wide_ref, qv_ref, up_b_ref,
-    out_ref, in_grad_ref, attn_s3, attn_r3, mlp_s3, mlp_r3, vec_g_ref,
-    qkv_f, proj_t, proj_f, up_f, down_f, vec_ref, vec_in, segk, segk_in, kv, kv_in, dkv, dkv_in,
+    sums_ref, attn_pair, mlp_pair,
+    qkv_f, proj_t, proj_f, up_f, down_f, vec_ref, vec_in, segk, segk_in, x_in, dkv, dkv_in,
     part, ar_send, ar_recv, ar_all,
     attn_g, up_g, down_g, attn_s1, attn_r1, attn_s2, attn_r2,
     mlp_s1, mlp_r1, mlp_s2, mlp_r2,
     vec_s, vec_r, send_sem, recv_sem,
 ):
+    attn_s3, attn_r3, mlp_s3, mlp_r3 = attn_pair.at[0], attn_pair.at[1], mlp_pair.at[0], mlp_pair.at[1]
     shard = lax.axis_index("shard")
     ctx = lax.axis_index("ctx")
     tp = lax.axis_index("tp")
@@ -508,7 +511,8 @@
     head_count = heads_width // 64
 
     barrier = pltpu.get_barrier_semaphore()
-    peers = [p1, p2, p3, pc] + [{"tp": t} for t in tps]
+    cross = [{"shard": index, "ctx": 1 - ctx} for index in (s1, s2, s3)]
+    peers = [p1, p2, p3, pc] + cross + [{"tp": t} for t in tps]
     for peer in peers:
         pl.semaphore_signal(barrier, inc=1, device_id=peer, device_id_type=MESH)
 
@@ -546,6 +550,7 @@
 
     qkv_far, qkv_near = gather_start(qkv_w, qkv_f)
     vec_copies = [send(vec_ref, vec_in.at[i], p) for i, p in enumerate((p1, p2, p3))]
+    x_copy = send(x_ref, x_in, pc)
     seg_copy = send(segk, segk_in, pc)
     qkv_f[shard] = qkv_w[...]
     proj_f[shard] = proj_t[...]
@@ -565,6 +570,9 @@
         return vec[index : index + 1, :size]
 
     normed_one = (unit_one * row(GAIN_ONE) + row(SHIFT_ONE)).astype(BF16)
+    x_copy.wait_recv()
+    unit_other, _ = unit_of(x_in[...].astype(F32))
+    normed_other = (unit_other * row(GAIN_ONE) + row(SHIFT_ONE)).astype(BF16)
     qkv_pass = gather_pass(qkv_f, qkv_far)
     proj_far, proj_near = gather_start(proj_t, proj_f)
     up_far, up_near = gather_start(up_w, up_f)
@@ -576,9 +584,8 @@
     )
     keys = mm(normed_one, weight_k).astype(BF16)
     values = (mm(normed_one, weight_v) + row(V_BIAS, heads_width)).astype(BF16)
-    kv[0] = keys
-    kv[1] = values
-    kv_copy = send(kv, kv_in, pc)
+    keys_other = mm(normed_other, weight_k).astype(BF16)
+    values_other = (mm(normed_other, weight_v) + row(V_BIAS, heads_width)).astype(BF16)
     queries = (mm(normed_one, weight_q) + row(Q_BIAS, heads_width)).astype(BF16)
 
     lane_head = lax.broadcasted_iota(jnp.int32, (tokens, heads_width), 1) // 64
@@ -599,9 +606,6 @@
         for i in range(head_count)
     ]
     proj_pass = gather_pass(proj_f, proj_far)
-    kv_copy.wait_recv()
-    keys_other = kv_in[0]
-    values_other = kv_in[1]
     probs_own, probs_other = [], []
     mixed_sum = jnp.zeros((tokens, heads_width), F32)
     for i in range(head_count):
@@ -709,6 +713,7 @@
     vec_s[0, PROJ_BIAS : PROJ_BIAS + 1, :] = column_sum(mid_grad)
     mid_grad_low = mid_grad.astype(BF16)
     mixed_grad = mm(mid_grad_low, weight_p).astype(BF16)
+    up_copy = reduce_two(up_copy, up_g, mlp_r1.at[0], mlp_s2.at[0], mlp_r2.at[0])
     delta_terms = mixed_grad.astype(F32) * mixed.astype(F32)
     zero = jnp.zeros((tokens, heads_width), F32)
     query_grad, key_own, value_own, key_other, value_other = zero, zero, zero, zero, zero
@@ -725,7 +730,9 @@
     dkv[0] = key_other.astype(BF16)
     dkv[1] = value_other.astype(BF16)
     dkv_copy = send(dkv, dkv_in, pc)
-    up_copy = reduce_two(up_copy, up_g, mlp_r1.at[0], mlp_s2.at[0], mlp_r2.at[0])
+    down_copy = reduce_three(
+        down_copy, down_g, mlp_r1.at[1], mlp_r2.at[1], mlp_s3.at[1], mlp_r3.at[1]
+    )
     out_sum = sum_pass(1, out_sum)
     proj_grad = mm(mid_grad_low, mixed, TN).reshape(4, depth, heads_width)
     for index in range(4):
@@ -746,32 +753,29 @@
         for block in range(4):
             attn_g[block, index] = weight_grad[block]
     attn_copy = reduce_one(attn_g, attn_s1, attn_r1)
+    up_copy = reduce_three(up_copy, up_g, mlp_r1.at[0], mlp_r2.at[0], mlp_s3.at[0], mlp_r3.at[0])
     one_sum = sum_pass(3, one_sum)
     attn_copy = reduce_two(attn_copy, attn_g, attn_r1, attn_s2, attn_r2)
-    down_copy = reduce_three(
-        down_copy, down_g, mlp_r1.at[1], mlp_r2.at[1], mlp_s3.at[1], mlp_r3.at[1]
-    )
-    up_copy = reduce_three(up_copy, up_g, mlp_r1.at[0], mlp_r2.at[0], mlp_s3.at[0], mlp_r3.at[0])
     norm_one_grad = sum_end(3, one_sum)
     vec_s[0, GAIN_ONE : GAIN_ONE + 1, :] = column_sum(norm_one_grad * unit_one)
     vec_s[0, SHIFT_ONE : SHIFT_ONE + 1, :] = column_sum(norm_one_grad)
-    vec_copy = send(vec_s.at[0], vec_r.at[0], p1)
+    place = ctx * 4 + shard
+    vec_copies = [send(vec_s.at[0], vec_r.at[place], p) for p in [p1, p2, p3, pc] + cross]
+    vec_r[place] = vec_s[0]
     attn_copy = reduce_three(attn_copy, attn_g, attn_r1, attn_r2, attn_s3, attn_r3)
-    in_grad_ref[...] = mid_grad + normalize_back(
+    sums_ref[tokens : 2 * tokens] = mid_grad + normalize_back(
         norm_one_grad, unit_one, inverse_one, row(GAIN_ONE)
     )
-    vec_copy.wait_recv()
-    vec_s[1] = vec_s[0] + vec_r[0]
-    vec_copy = send(vec_s.at[1], vec_r.at[1], p2)
-    out_ref[...] = residual_mid + sum_end(1, out_sum) + row(DOWN_BIAS)
-    vec_copy.wait_recv()
-    vec_s[2] = vec_s[1] + vec_r[1]
-    vec_copy = send(vec_s.at[2], vec_r.at[2], pc)
+    sums_ref[0:tokens] = residual_mid + sum_end(1, out_sum) + row(DOWN_BIAS)
+    for copy in vec_copies:
+        copy.wait_recv()
+    vec_total = vec_r[0]
+    for index in range(1, 8):
+        vec_total = vec_total + vec_r[index]
+    sums_ref[2 * tokens : 2 * tokens + VEC_ROWS] = vec_total
     down_copy.wait_recv()
     up_copy.wait_recv()
     attn_copy.wait_recv()
-    vec_copy.wait_recv()
-    vec_g_ref[...] = vec_s[2] + vec_r[2]
     for copy in started:
         copy.wait_send()
 
@@ -795,13 +799,9 @@
     vmem = pltpu.VMEM
     shaped = jax.ShapeDtypeStruct
     middle_shapes = (
-        shaped((tokens, width), F32),
-        shaped((tokens, width), F32),
-        shaped(attn_shape, BF16),
-        shaped(attn_shape, BF16),
-        shaped((2,) + mlp_shape, BF16),
-        shaped((2,) + mlp_shape, BF16),
-        shaped((VEC_ROWS, width), F32),
+        shaped((2 * tokens + VEC_ROWS, width), F32),
+        shaped((2,) + attn_shape, BF16),
+        shaped((2, 2) + mlp_shape, BF16),
     )
     proj_shape = (depth, heads_width)
     qkv_shape = (3, depth, heads_width)
@@ -810,7 +810,7 @@
         vmem((4,) + mlp_shape, BF16), vmem((4,) + mlp_shape, BF16),
         vmem((VEC_ROWS, width), F32), vmem((3, VEC_ROWS, width), F32),
         vmem((8, tokens), jnp.int32), vmem((8, tokens), jnp.int32),
-        vmem((2, tokens, heads_width), BF16), vmem((2, tokens, heads_width), BF16),
+        vmem((tokens, width), BF16),
         vmem((2, tokens, heads_width), BF16), vmem((2, tokens, heads_width), BF16),
         vmem((4, 4, tokens // 4, width), F32), vmem((4, 4, tokens // 4, width), BF16),
         vmem((4, 3, tokens // 4, width), BF16), vmem((4, 4, tokens // 4, width), BF16),
@@ -819,7 +819,7 @@
         vmem(attn_shape, BF16), vmem(attn_shape, BF16),
         vmem((2, 2) + mlp_shape, BF16), vmem((2, 2) + mlp_shape, BF16),
         vmem((2,) + mlp_shape, BF16), vmem((2,) + mlp_shape, BF16),
-        vmem((3, VEC_ROWS, width), F32), vmem((3, VEC_ROWS, width), F32),
+        vmem((1, VEC_ROWS, width), F32), vmem((8, VEC_ROWS, width), F32),
         pltpu.SemaphoreType.DMA((COPIES,)), pltpu.SemaphoreType.DMA((COPIES,)),
     ]
     whole = pl.BlockSpec(memory_space=pltpu.VMEM)
@@ -827,7 +827,7 @@
         block_kernel,
         out_shape=middle_shapes,
         in_specs=[whole] * 10,
-        out_specs=(whole,) * 7,
+        out_specs=(whole,) * 3,
         scratch_shapes=scratch,
         compiler_params=pltpu.CompilerParams(
             collective_id=0, has_side_effects=True, vmem_limit_bytes=VMEM_LIMIT
@@ -849,7 +849,7 @@
     ) = pl.pallas_call(
         finish_kernel,
         out_shape=result_shapes,
-        in_specs=[whole] * 7,
+        in_specs=[whole] * 3,
         out_specs=(whole,) * 14,
         compiler_params=pltpu.CompilerParams(vmem_limit_bytes=16 * 1024 * 1024),
     )(*middle)

time: 99.3 us -> 93 us (0.937)
  local copies, waits for them, and re-layouts: 10.8 us -> 3.55 us
  other arithmetic: 0.71 us -> 4.64 us
  Pallas kernels: 86.6 us -> 83.8 us
    unnamed x26 -> x6, local copies, waits for them, and re-layouts: 10.8 us -> 3.55 us
    convert_element_type x6, other arithmetic: 0.02 us -> 3.94 us  [paired_body(): wide = jnp.where(at_row == index, vector.astype(F32)[None, :], wide)]
    pallas_call x1, Pallas kernels: 84.8 us -> 82.1 us  [paired_body(): pl.pallas_call(block_kernel, out_shape=middle_shapes, in_specs=[whole] *...]
where the time goes in v3:
time: 93 us; the launch traced here: 92.7 us
  Pallas kernels  83.8 us (90%)
  other arithmetic  4.64 us (5%)
  local copies, waits for them, and re-layouts  3.55 us (4%)
    pallas_call x1, Pallas kernels, paired_body(): pl.pallas_call(block_kernel, out_shape=middle_shapes, in_specs=[whole] *...  82.1 us
    convert_element_type x6, other arithmetic, paired_body(): wide = jnp.where(at_row == index, vector.astype(F32)[None, :], wide)  3.94 us
    unnamed x6, local copies, waits for them, and re-layouts  3.55 us

profile of v3, /device:TPU:0, one launch (start us, length us, event | category | flops | bytes accessed | tf_op | source)
XLA Modules:
  0.0 92.7 jit_solution(13481635932228657183)
XLA Ops:
  0.6 0.7 convert_element_type.23
  1.3 0.7 convert_element_type.22
  2.0 0.7 convert_element_type.21
  2.6 0.7 convert_element_type.20
  3.3 0.7 convert_element_type.19
  3.9 0.7 convert_element_type.18
  4.6 0.7 select_select_fusion.wide_ref
  5.3 82.1 %shard_map.254 = (f32[272,768]{1,0:T(8,128)}, bf16[2,4,192,192]{3,2,1,0:T(8,128)(2,1)}, bf16[2,2,192,768]{3,2,1,0:T(8,128)(2,1)}) custom-call(bf16[128,768]{1,0:T(8,128)(2,1)} %bitcast.18, bf16[128,768]{1,0:T(8,128)(2,1)} %bitcast.19, s32[1,128]{1,0:T(1,128)} %seg_ref.1, bf16[3,192,192]{2,1,0:T(8,128)(2,1)} %bitcast.16, bf16[192,192]{1,0:T(8,128)(2,1)} %proj_w.1, ...), custom_call_target="tpu_custom_call" | custom-call | tf_op jit(solution)/shard_map/pallas_call | solution.py:826
  87.4 0.0 copy-start
  87.4 1.3 %copy-done = bf16[2,2,192,768]{3,2,1,0:T(8,128)(2,1)S(1)} copy-done((bf16[2,2,192,768]{3,2,1,0:T(8,128)(2,1)S(1)}, bf16[2,2,192,768]{3,2,1,0:T(8,128)(2,1)}, u32[]{:S(2)}) %copy-start) | copy-done | bytes 1179672
  88.7 0.0 copy-start.1
  88.7 1.1 %copy-done.1 = f32[272,768]{1,0:T(8,128)S(1)} copy-done((f32[272,768]{1,0:T(8,128)S(1)}, f32[272,768]{1,0:T(8,128)}, u32[]{:S(2)}) %copy-start.1) | copy-done | bytes 835608
  89.8 0.0 copy-start.2
  89.8 1.1 %copy-done.2 = bf16[2,4,192,192]{3,2,1,0:T(8,128)(2,1)S(1)} copy-done((bf16[2,4,192,192]{3,2,1,0:T(8,128)(2,1)S(1)}, bf16[2,4,192,192]{3,2,1,0:T(8,128)(2,1)}, u32[]{:S(2)}) %copy-start.2) | copy-done | bytes 589848
  91.0 1.7 %shard_map.255 = (f32[128,768]{1,0:T(8,128)}, f32[128,768]{1,0:T(8,128)}, f32[3,192,192]{2,1,0:T(8,128)}, f32[192,192]{1,0:T(8,128)}, f32[192,768]{1,0:T(8,128)}...) custom-call(f32[272,768]{1,0:T(8,128)S(1)} %copy-done.1, ...), custom_call_target="tpu_custom_call" | custom-call | tf_op jit(solution)/shard_map/pallas_call | solution.py:849
  (3 shorter events, 0.0 us)
Async XLA Ops:
  87.4 1.3 %copy-start = (bf16[2,2,192,768]{3,2,1,0:T(8,128)(2,1)S(1)}, bf16[2,2,192,768]{3,2,1,0:T(8,128)(2,1)}, u32[]{:S(2)}) copy-start(bf16[2,2,192,768]{3,2,1,0:T(8,128)(2,1)} %get-tuple-element.33.mlp_pair) | copy-start | bytes 3538948
  88.7 1.1 %copy-start.1 = (f32[272,768]{1,0:T(8,128)S(1)}, f32[272,768]{1,0:T(8,128)}, u32[]{:S(2)}) copy-start(f32[272,768]{1,0:T(8,128)} %get-tuple-element.31.sums_ref) | copy-start | bytes 2506756
  89.8 1.1 %copy-start.2 = (bf16[2,4,192,192]{3,2,1,0:T(8,128)(2,1)S(1)}, bf16[2,4,192,192]{3,2,1,0:T(8,128)(2,1)}, u32[]{:S(2)}) copy-start(bf16[2,4,192,192]{3,2,1,0:T(8,128)(2,1)} %get-tuple-element.32.attn_pair) | copy-start | bytes 1769476
